TPU v7x, 128 devices: a whole 4x4x4 slice. The times are simulated.
128 devices in a mesh: tok: 4 (over z), ep: 32 (over y, x, core).
Axes of the slice: x: 4, y: 4, z: 4, core: 2. Of those that a mesh axis runs over, the one named last changes fastest.
Arguments:
- resid: bfloat16 [16384, 2048], P(('tok', 'ep')), may hold values from -6 to 6
- qkv: bfloat16 [16384, 5120], P(('tok', 'ep')), may hold values from -8 to 8
- cache_kv: bfloat16 [128, 4, 64, 256], P('ep', 'tok'), may hold values from -6 to 6
- page_slot: int32 [128], P('ep'), may hold values from 0 to 127, each once
- seg_lengths: int32 [16], replicated, may hold values from 1 to 2048, 16384 in all
- cache_age: int32 [16], replicated, may hold values from 0 to 512, as said below
- w_out: bfloat16 [4096, 2048], P('tok'), may hold values from -0.09375 to 0.09375
- norm_gain: float32 [2048], replicated, may hold values from 0.1 to 1.9
- routes: int32 [16384, 8], P(('tok', 'ep')), may hold values from 0 to 127, all different within a row; in each aligned block of 128 rows (0 to 127, 128 to 255, ...) at most 16 rows name the same one
- route_probs: float32 [16384, 8], P(('tok', 'ep')), may hold values from 0.05 to 1
- w_gate_up: bfloat16 [128, 2048, 1536], P(('tok', 'ep')), may hold values from -0.125 to 0.125
- w_down: bfloat16 [128, 768, 2048], P(('tok', 'ep')), may hold values from -0.21875 to 0.21875
Outputs:
- layer_out: bfloat16 [16384, 2048], P(('tok', 'ep'))
Inputs may be any that keep to these rules, and one draw needn't show every extreme that they name: `routes`: in each aligned block of 128 rows (the rows of one shard) no expert is named more than 16 times, a bound that some block reaches. `cache_age`: exactly 5 segments have no cache; some segment has 512 cached positions. `page_slot`: logical page l is page l % 8 of segment l // 8.
All inputs are finite; a program needn't handle non-finite values.
Results may differ from a plain program's by a relative error of at most 0.015.
Values may be sent and summed in bfloat16 or wider, within the bound.
A program may use at most 128 MiB of HBM per device.

v0:
```python
import math

import jax
import jax.numpy as jnp
from jax import lax
from jax.sharding import PartitionSpec as P

D = 2048
FF = 768
HEAD = 128
QPG = 8
TOP = 8
PAGE = 64
SEG_PAGES = 8


NEG_FILL = -1e30
NORM_EPS = 1e-06


def segment_meta(tok_rows, seg_lengths, cache_age):
    seg_ends = jnp.cumsum(seg_lengths)
    seg_starts = seg_ends - seg_lengths
    segment = jnp.sum((tok_rows[:, None] >= seg_ends[None, :]).astype(jnp.int32), axis=1)
    matched = segment[:, None] == jnp.arange(seg_lengths.shape[0], dtype=jnp.int32)[None, :]
    first_row = jnp.sum(jnp.where(matched, seg_starts[None, :], 0), axis=1)
    seg_age = jnp.sum(jnp.where(matched, cache_age[None, :], 0), axis=1)
    return (segment, tok_rows - first_row + seg_age)


def region_update(states, scores, allowed, value_rows):
    running, denom, summed = states
    scores = jnp.where(allowed, scores, NEG_FILL)
    newest = jnp.maximum(running, jnp.max(scores, axis=-1))
    weights = jnp.where(allowed, jnp.exp(scores - newest[:, None]), 0.0)
    factor = jnp.exp(running - newest)
    denom = denom * factor + jnp.sum(weights, axis=-1)
    summed = summed * factor[:, None] + jnp.dot(
        weights.astype(jnp.bfloat16), value_rows, preferred_element_type=jnp.float32
    )
    return (newest, denom, summed)


def expert_rows(arrived, w_gate_up, w_down):
    shaped = arrived.shape
    flat_rows = arrived.reshape(-1, shaped[-1])
    projected = jnp.dot(flat_rows, w_gate_up[0], preferred_element_type=jnp.float32)
    hidden = (jax.nn.silu(projected[:, :FF]) * projected[:, FF:]).astype(jnp.bfloat16)
    produced = jnp.dot(hidden, w_down[0], preferred_element_type=jnp.float32).astype(jnp.bfloat16)
    return produced.reshape(shaped)


def on_device(
    resid,
    qkv,
    cache_kv,
    page_slot,
    seg_lengths,
    cache_age,
    w_out,
    norm_gain,
    routes,
    route_probs,
    w_gate_up,
    w_down,
):
    tok_groups = lax.axis_size("tok")
    ep_count = lax.axis_size("ep")
    member = lax.axis_index("ep")
    tok_dev = resid.shape[0]
    q_width = QPG * HEAD
    scale = 1.0 / math.sqrt(HEAD)
    grouped = lax.all_to_all(qkv, "tok", split_axis=1, concat_axis=0, tiled=True)
    queries = grouped[:, :q_width]
    own_keys = grouped[:, q_width:]
    local_rows = jnp.arange(tok_groups * tok_dev, dtype=jnp.int32)
    global_rows = (local_rows // tok_dev * ep_count + member) * tok_dev + local_rows % tok_dev
    q_segment, q_position = segment_meta(global_rows, seg_lengths, cache_age)
    seg_count = seg_lengths.shape[0]
    page_count = cache_kv.shape[0]
    page_seg = page_slot // SEG_PAGES
    page_first = page_slot % SEG_PAGES * PAGE
    page_match = page_seg[:, None] == jnp.arange(seg_count, dtype=jnp.int32)[None, :]
    page_age = jnp.sum(jnp.where(page_match, cache_age[None, :], 0), axis=1)
    slot_position = page_first[:, None] + jnp.arange(PAGE, dtype=jnp.int32)[None, :]
    slot_segment = jnp.where(slot_position < page_age[:, None], page_seg[:, None], -1)
    cached_rows = cache_kv.reshape(page_count * PAGE, 2 * HEAD)
    cached_segment = slot_segment.reshape(-1)
    cached_position = slot_position.reshape(-1)
    region_rows = tok_dev * QPG
    query_blocks = queries.reshape(tok_groups, region_rows, HEAD)
    seg_blocks = q_segment.reshape(tok_groups, tok_dev)
    pos_blocks = q_position.reshape(tok_groups, tok_dev)
    start_state = tuple(
        (
            (
                jnp.full((region_rows,), NEG_FILL, jnp.float32),
                jnp.zeros((region_rows,), jnp.float32),
                jnp.zeros((region_rows, HEAD), jnp.float32),
            )
            for region in range(tok_groups)
        )
    )
    bank_rows = jnp.concatenate([own_keys, cached_rows], axis=0)
    bank_segment = jnp.concatenate([q_segment, cached_segment])
    bank_position = jnp.concatenate([q_position, cached_position])
    states = start_state
    piece_rows = lax.all_gather(bank_rows, "ep", axis=0, tiled=True)
    piece_segment = lax.all_gather(bank_segment, "ep", axis=0, tiled=True)
    piece_position = lax.all_gather(bank_position, "ep", axis=0, tiled=True)
    key_block = math.gcd(piece_rows.shape[0], 256)
    steps_count = piece_rows.shape[0] // key_block

    def visit(current, blocks):
        block_rows, block_segment, block_position = blocks
        key_rows = block_rows[:, :HEAD]
        value_rows = block_rows[:, HEAD:]
        updated = []
        for region in range(tok_groups):
            allowed = (seg_blocks[region][:, None] == block_segment[None, :]) & (
                block_position[None, :] <= pos_blocks[region][:, None]
            )

            def attend(state_now, allowed=allowed, region=region):
                scores = (
                    jnp.einsum(
                        "rd,kd->rk",
                        query_blocks[region],
                        key_rows,
                        preferred_element_type=jnp.float32,
                    )
                    * scale
                )
                widened = jnp.repeat(allowed, QPG, axis=0)
                return region_update(state_now, scores, widened, value_rows)

            updated.append(
                lax.cond(jnp.any(allowed), attend, lambda state_now: state_now, current[region])
            )
        return (tuple(updated), None)

    blocks = (
        piece_rows.reshape(steps_count, key_block, 2 * HEAD),
        piece_segment.reshape(steps_count, key_block),
        piece_position.reshape(steps_count, key_block),
    )
    states, ignored = lax.scan(visit, states, blocks)
    attended = jnp.concatenate(
        [(summed / denom[:, None]).reshape(tok_dev, q_width) for running, denom, summed in states],
        axis=0,
    ).astype(jnp.bfloat16)
    attn_sum = lax.psum_scatter(
        jnp.dot(attended, w_out, preferred_element_type=jnp.float32).astype(jnp.bfloat16),
        "tok",
        scatter_dimension=0,
        tiled=True,
    ).astype(jnp.float32)
    mixed = (resid.astype(jnp.float32) + attn_sum).astype(jnp.bfloat16)
    widened_mix = mixed.astype(jnp.float32)
    normed = (
        widened_mix
        * lax.rsqrt(jnp.mean(widened_mix * widened_mix, axis=-1, keepdims=True) + NORM_EPS)
        * norm_gain[None, :]
    ).astype(jnp.bfloat16)
    expert_count = tok_groups * ep_count
    capacity = max(2, 2 * tok_dev * TOP // expert_count)
    flat_route = routes.reshape(-1)
    one_hot = (flat_route[:, None] == jnp.arange(expert_count, dtype=jnp.int32)[None, :]).astype(
        jnp.int32
    )
    earlier = jnp.cumsum(one_hot, axis=0) - one_hot
    slot_rank = jnp.sum(earlier * one_hot, axis=1)
    slot_index = flat_route * capacity + slot_rank
    source_row = (
        jnp.full((expert_count * capacity,), tok_dev, jnp.int32)
        .at[slot_index]
        .set(jnp.arange(tok_dev * TOP, dtype=jnp.int32) // TOP)
    )
    padded = jnp.concatenate([normed, jnp.zeros((1, D), jnp.bfloat16)], axis=0)
    outgoing = padded[source_row].reshape(expert_count, capacity, D)
    returned = lax.all_to_all(
        expert_rows(
            lax.all_to_all(outgoing, ("tok", "ep"), split_axis=0, concat_axis=0, tiled=True),
            w_gate_up,
            w_down,
        ),
        ("tok", "ep"),
        split_axis=0,
        concat_axis=0,
        tiled=True,
    ).reshape(expert_count * capacity, D)
    picked = returned[slot_index].reshape(tok_dev, TOP, D)
    shares = route_probs / jnp.sum(route_probs, axis=1, keepdims=True)
    routed = jnp.einsum("tk,tkd->td", shares, picked, preferred_element_type=jnp.float32)
    return (widened_mix + routed).astype(jnp.bfloat16)


def solution(mesh):
    placed = (
        P(("tok", "ep"), None),
        P(("tok", "ep"), None),
        P("ep", "tok", None, None),
        P("ep"),
        P(),
        P(),
        P("tok", None),
        P(),
        P(("tok", "ep"), None),
        P(("tok", "ep"), None),
        P(("tok", "ep"), None, None),
        P(("tok", "ep"), None, None),
    )
    return jax.shard_map(
        on_device, mesh=mesh, in_specs=placed, out_specs=P(("tok", "ep"), None), check_vma=False
    )
```

profile of v0, /device:TPU:8, one launch (start us, length us, event | category | flops | bytes accessed | tf_op | source)
XLA Modules:
  0.0 1234.1 jit_solution(14769746627277305957)
XLA Ops:
  11.6 23.2 %all_to_all.29 = bf16[128,4,1280]{2,0,1:T(8,128)(2,1)S(1)} all-to-all(bf16[128,4,1280]{2,0,1:T(8,128)(2,1)} %copy.70), channel_id=1, replica_groups=mesh['tok'=4,'ep'=32] {'tok'}, dimensions={1} | all-to-all | bytes 2621440 | tf_op jit(solution)/shard_map/all_to_all | solution.py:73
  37.5 24.5 %all-gather.1 = s32[32,1,768]{2,1,0:T(1,128)S(1)} all-gather(s32[1,1,768]{2,1,0:T(1,128)S(1)} %reshape.258), channel_id=1, replica_groups=mesh['tok'=4,'ep'=32] {'ep'}, dimensions={0}, use_global_device_ids=true | all-gather | bytes 101376 | tf_op jit(solution)/shard_map/all_gather | solution.py:110
  62.8 22.4 %all-gather = s32[32,1,768]{2,1,0:T(1,128)S(1)} all-gather(s32[1,1,768]{2,1,0:T(1,128)S(1)} %reshape.256), channel_id=1, replica_groups=mesh['tok'=4,'ep'=32] {'ep'}, dimensions={0}, use_global_device_ids=true | all-gather | bytes 101376 | tf_op jit(solution)/shard_map/all_gather | solution.py:109
  90.7 8.7 all-gather.4.cloned.1.call-done
  102.8 726.8 %while.32 = (s32[]{:T(128)}, f32[1024]{0:T(1024)S(1)}, f32[1024]{0:T(1024)S(1)}, f32[1024,128]{1,0:T(8,128)}, f32[1024]{0:T(1024)S(1)}, /*index=5*/f32[1024]{0:T...) while((s32[]{:T(128)}, f32[1024]{0:T(1024)S(1)}, ...), condition=%wide.region_26.27_spmd, body=%wide.region_5.26_spmd.sunk | while | flops 547889152 | bytes 25709204 | solution.py:147
  116.3 4.4 conditional.10
  125.9 4.4 conditional.10
  145.1 4.4 conditional.10
  155.4 4.4 conditional.11
  174.0 4.4 conditional.10
  198.4 4.4 conditional.10
  227.2 4.4 conditional.10
  247.8 4.4 conditional.8
  256.0 4.4 conditional.10
  276.6 4.4 conditional.8
  284.8 4.4 conditional.10
  289.9 4.4 conditional.11
  322.3 4.4 conditional.10
  327.4 4.4 conditional.11
  336.3 4.4 conditional.10
  355.9 4.4 conditional.8
  364.2 4.4 conditional.10
  369.2 4.4 conditional.11
  378.9 4.4 conditional.11
  434.9 4.4 conditional.11
  470.9 4.4 conditional.11
  475.9 4.4 conditional.8
  494.6 4.4 conditional.10
  500.4 4.4 conditional.8
  552.0 4.4 conditional.8
  623.2 4.4 conditional.11
  664.1 4.4 conditional.8
  688.6 4.4 conditional.8
  780.1 4.4 conditional.10
  795.0 4.4 conditional.10
  804.6 4.4 conditional.10
  819.5 4.4 conditional.10
  825.2 4.4 conditional.8
  839.2 6.2 convolution_convert_fusion.1
  850.5 4.5 scatter_custom_fusion
  855.0 99.6 %reduce-scatter.2.cloned.1.call-done = bf16[128,2048]{1,0:T(8,128)(2,1)} async-done(((bf16[512,2048]{1,0:T(8,128)(2,1)}), bf16[128,2048]{1,0:T(8,128)(2,1)}) %reduce-scatter.2.cloned.1.call-update) | async-done | bytes 524304 | tf_op jit(solution)/shard_map/reduce_scatter | solution.py:152
  958.4 17.5 %gather_fusion = bf16[2048,2048]{1,0:T(8,128)(2,1)} fusion(bf16[129,2048]{1,0:T(8,128)(2,1)} %concatenate.20, s32[2048]{0:T(1024)S(1)} %fusion.60), kind=kCustom, calls=%fused_computation | custom fusion | bytes 16785408 | tf_op jit(solution)/shard_map/gather | solution.py:180
  975.8 104.7 %all_to_all.30 = bf16[128,16,2048]{2,1,0:T(8,128)(2,1)S(1)} all-to-all(bf16[128,16,2048]{2,1,0:T(8,128)(2,1)} %bitcast.108), channel_id=1, replica_groups=mesh['tok'=4,'ep'=32] {'tok','ep'}, dimensions={0} | all-to-all | bytes 16777216 | tf_op jit(solution)/shard_map/all_to_all | solution.py:183
  1080.5 15.8 %fusion.37 = f32[2048,1536]{1,0:T(8,128)S(1)} fusion(bf16[2048,2048]{1,0:T(8,128)(2,1)S(1)} %bitcast.110, bf16[1,2048,1536]{2,1,0:T(8,128)(2,1)} %param.32), kind=kOutput, calls=%fused_computation.77 | convolution fusion | flops 12884901888 | bytes 27262976 | tf_op jit(solution)/shard_map/dot_general | solution.py:47
  1096.3 8.9 convolution_convert_fusion
  1105.2 6.8 all-to-all-start.2
  1112.2 95.9 %all-to-all-done.2 = bf16[128,16,2048]{2,1,0:T(8,128)(2,1)} async-done(((bf16[128,16,2048]{2,1,0:T(8,128)(2,1)}), bf16[128,16,2048]{2,1,0:T(8,128)(2,1)}, u32[]{:S(2)}, u32[]{:S(2)}) %all-to-all-start.2) | async-done | bytes 8388640 | tf_op jit(solution)/shard_map/all_to_all | solution.py:181
  1208.1 13.3 %gather_fusion.1 = bf16[1024,2048]{1,0:T(8,128)(2,1)} fusion(bf16[2048,2048]{1,0:T(8,128)(2,1)} %bitcast.40, s32[1024]{0:T(1024)S(1)} %broadcast_clamp_fusion), kind=kCustom, calls=%fused_computation.1 | custom fusion | bytes 8392704 | tf_op jit(solution)/shard_map/gather | solution.py:192
  (1340 shorter events, 590.7 us)
Async XLA Ops:
  6.5 1089.7 %copy-start = (bf16[1,768,2048]{2,1,0:T(8,128)(2,1)S(1)}, bf16[1,768,2048]{2,1,0:T(8,128)(2,1)}, u32[]{:S(2)}) copy-start(bf16[1,768,2048]{2,1,0:T(8,128)(2,1)} %param.33) | copy-start | bytes 9437188
  6.5 29.5 %copy-start.3 = (bf16[4,1,64,256]{3,2,1,0:T(8,128)(2,1)S(1)}, bf16[4,1,64,256]{3,2,1,0:T(8,128)(2,1)}, u32[]{:S(2)}) copy-start(bf16[4,1,64,256]{3,2,1,0:T(8,128)(2,1)} %param.24) | copy-start | bytes 393220
  6.5 30.3 %copy-start.8 = (s32[16]{0:T(128)S(1)}, s32[16]{0:T(128)}, u32[]{:S(2)}) copy-start(s32[16]{0:T(128)} %param.26) | copy-start | bytes 196
  6.5 30.6 %copy-start.9 = (s32[4]{0:T(128)S(1)}, s32[4]{0:T(128)}, u32[]{:S(2)}) copy-start(s32[4]{0:T(128)} %param.25) | copy-start | bytes 52
  6.5 30.8 %copy-start.7 = (s32[16]{0:T(128)S(1)}, s32[16]{0:T(128)}, u32[]{:S(2)}) copy-start(s32[16]{0:T(128)} %param.27) | copy-start | bytes 196
  6.5 92.8 %all-gather.4.cloned.1.call-start = ((), (), s32[]{:S(2)}) async-start(), calls=%async_computation.4 | async-start | bytes 12976128 | tf_op jit(solution)/shard_map/all_gather | solution.py:108
  34.8 1.1 copy-start.1
  36.8 917.8 %reduce-scatter.2.cloned.1.call-start = ((), (), s32[]{:S(2)}) async-start(), calls=%async_computation.5 | async-start | bytes 2621440 | tf_op jit(solution)/shard_map/reduce_scatter | solution.py:152
  839.2 6.3 copy-start.4
  845.4 110.7 %copy-start.6 = (f32[2048]{0:T(1024)S(1)}, f32[2048]{0:T(1024)}, u32[]{:S(2)}) copy-start(f32[2048]{0:T(1024)} %param.29) | copy-start | bytes 24580
  846.0 0.8 copy-start.2
  1105.2 6.8 copy-start.5
  1105.2 102.8 %all-to-all-start.2 = ((bf16[128,16,2048]{2,1,0:T(8,128)(2,1)}), bf16[128,16,2048]{2,1,0:T(8,128)(2,1)}, u32[]{:S(2)}, u32[]{:S(2)}) async-start(bf16[128,16,2048]{2,1,0:T(8,128)(2,1)} %bitcast.109), calls=%async_computation.3 | async-start | bytes 16777216 | tf_op jit(solution)/shard_map/all_to_all | solution.py:181
Sparse Core Ops, SparseCore 0:
  36.9 62.4 all-gather.3
  845.5 108.9 reduce-scatter.1
where the time goes:
time: 1260 us; the launch traced here: 1230 us
  loops' own time  261 us (21%)
  local copies, waits for them, and re-layouts  241 us (19%)
  matrix products  216 us (17%)
  waiting for transfers between devices  204 us (16%)
  blocking collectives  175 us (14%)
  other arithmetic  116 us (9%)
  between operations  13.7 us (1%)
    another operation x1, loops' own time, on_device(): states, ignored = lax.scan(visit, states, blocks)  253 us
    dot_general x51, matrix products, region_update(): jnp.dot(weights.astype(jnp.bfloat16), value_rows, preferred_element_type=...  116 us
    all_to_all x1, blocking collectives, on_device(): lax.all_to_all(outgoing, ('tok', 'ep'), split_axis=0, concat_axis=0, tile...  105 us
    reduce_scatter x1, waiting for transfers between devices, on_device(): lax.psum_scatter(jnp.dot(attended, w_out, preferred_element_type=jnp.floa...  99.6 us
    all_to_all x1, waiting for transfers between devices, on_device(): lax.all_to_all(expert_rows(lax.all_to_all(outgoing, ('tok', 'ep'), split_...  95.9 us
    reduce_or x96, other arithmetic, visit(): jnp.any(allowed)  88.2 us
    squeeze x96, local copies, waits for them, and re-layouts, on_device(): states, ignored = lax.scan(visit, states, blocks)  87.6 us
    dynamic_slice x96, local copies, waits for them, and re-layouts, on_device(): states, ignored = lax.scan(visit, states, blocks)  68.1 us
  transfers between devices with their start and end apart: 3, of which 3 were waited for; matrix products, arithmetic and copies ran while one was open for 1% of the time, Pallas kernels for 0%

commit v1 on v0

v1 whole, which is shorter than its diff:
```python
import functools
import math

import jax
import jax.numpy as jnp
from jax import lax
from jax.experimental import pallas as pl
from jax.experimental.pallas import tpu as pltpu
from jax.sharding import PartitionSpec as P

D = 2048
FF = 768
HEAD = 128
QPG = 8
TOP = 8
PAGE = 64
SEG_PAGES = 8
SEG_MOST = 2048
STEP = 256
META_ROWS = 16


NEG_FILL = -1e30
NORM_EPS = 1e-06


def attention_kernel(tok_dev, segs, most_steps, seg_ref, row_ref, q_ref, bank_ref, out_ref, score_ref, low_ref, top_ref, den_ref, acc_ref):
    rows = tok_dev * QPG
    pages = segs * SEG_PAGES
    rate = math.log2(math.e) / math.sqrt(HEAD)

    def tiled(mask):
        return jnp.concatenate([mask] * QPG, axis=0)

    def one_block(block, carry):
        first = seg_ref[3 * segs + block]
        last = first + tok_dev - 1
        token = first + lax.broadcasted_iota(jnp.int32, (tok_dev, STEP), 0)
        column = lax.broadcasted_iota(jnp.int32, (tok_dev, STEP), 1)
        low = jnp.zeros((tok_dev, STEP), jnp.int32)
        begin = jnp.int32(0)
        for s in range(segs):
            start = seg_ref[s]
            low = jnp.where(token >= start, start, low)
            begin = jnp.where(first >= start, start, begin)
        low_ref[...] = low
        query = jnp.concatenate([q_ref[block, :, h * HEAD:(h + 1) * HEAD] for h in range(QPG)], axis=0)
        den_ref[...] = jnp.zeros_like(den_ref)
        acc_ref[...] = jnp.zeros_like(acc_ref)

        def region(steps, bank_of, mask_of, opening):
            if opening:
                held = jnp.full((rows, HEAD), NEG_FILL, jnp.float32)
            else:
                held = top_ref[...]

            def score(step, running):
                keys = jnp.concatenate([bank_ref[pl.ds(at, size), :HEAD] for at, size in bank_of(step)], axis=0)
                scores = lax.dot_general(query, keys, (((1,), (1,)), ((), ())), preferred_element_type=jnp.float32) * rate
                scores = jnp.where(tiled(mask_of(step)), scores, NEG_FILL)
                score_ref[step] = scores
                return jnp.maximum(running, jnp.maximum(scores[:, :HEAD], scores[:, HEAD:]))

            newest = lax.fori_loop(0, steps, score, held)
            newest = jnp.broadcast_to(jnp.max(newest, axis=1, keepdims=True), (rows, HEAD))
            if not opening:
                factor = jnp.exp2(held - newest)
                den_ref[...] = den_ref[...] * factor
                acc_ref[...] = acc_ref[...] * factor
            top_ref[...] = newest

            def weigh(step, ignored):
                top = top_ref[...]
                weights = jnp.exp2(score_ref[step] - jnp.concatenate([top, top], axis=1))
                den_ref[...] += weights[:, :HEAD] + weights[:, HEAD:]
                values = jnp.concatenate([bank_ref[pl.ds(at, size), HEAD:] for at, size in bank_of(step)], axis=0)
                acc_ref[...] += jnp.dot(weights.astype(jnp.bfloat16), values, preferred_element_type=jnp.float32)
                return ignored

            lax.fori_loop(0, steps, weigh, 0)

        chunk_last = first // tok_dev
        chunk_first = begin // tok_dev
        steps = (chunk_last - chunk_first + 2) // 2

        def new_chunk(step, half):
            return chunk_last - 2 * step - 1 + half

        def new_bank(step):
            return [(pl.multiple_of(row_ref[pages + jnp.maximum(new_chunk(step, half), 0)], 16), tok_dev) for half in range(2)]

        def new_mask(step):
            key = new_chunk(step, 0) * tok_dev + column
            return (key >= low_ref[...]) & (key <= token)

        region(steps, new_bank, new_mask, True)

        def cached(s, ignored):
            start, end, age = seg_ref[s], seg_ref[segs + s], seg_ref[2 * segs + s]

            @pl.when((start <= last) & (end > first) & (age > 0))
            def _():
                def page_bank(step):
                    return [(pl.multiple_of(row_ref[s * SEG_PAGES + step * (STEP // PAGE) + part], 16), PAGE) for part in range(STEP // PAGE)]

                def page_mask(step):
                    return (token >= start) & (token < end) & (step * STEP + column < age)

                region((age + STEP - 1) // STEP, page_bank, page_mask, False)
            return ignored

        lax.fori_loop(0, segs, cached, 0)
        total = jnp.sum(den_ref[...], axis=1, keepdims=True)
        result = (acc_ref[...] / total).astype(jnp.bfloat16)
        for h in range(QPG):
            out_ref[block, :, h * HEAD:(h + 1) * HEAD] = result[h * tok_dev:(h + 1) * tok_dev]
        return carry

    lax.fori_loop(0, q_ref.shape[0], one_block, 0)


def attention(seg_table, row_table, queries, bank, segs, seg_most):
    blocks, tok_dev, width = queries.shape
    most_steps = max((seg_most + tok_dev) // tok_dev // 2 + 1, SEG_PAGES * PAGE // STEP)
    rows = tok_dev * QPG
    return pl.pallas_call(
        functools.partial(attention_kernel, tok_dev, segs, most_steps),
        out_shape=jax.ShapeDtypeStruct(queries.shape, jnp.bfloat16),
        in_specs=[pl.BlockSpec(memory_space=pltpu.SMEM)] * 2 + [pl.BlockSpec(memory_space=pltpu.VMEM)] * 2,
        out_specs=pl.BlockSpec(memory_space=pltpu.VMEM),
        scratch_shapes=[
            pltpu.VMEM((most_steps, rows, STEP), jnp.float32),
            pltpu.VMEM((tok_dev, STEP), jnp.int32),
            pltpu.VMEM((rows, HEAD), jnp.float32),
            pltpu.VMEM((rows, HEAD), jnp.float32),
            pltpu.VMEM((rows, HEAD), jnp.float32),
        ],
        compiler_params=pltpu.CompilerParams(vmem_limit_bytes=48 << 20),
        name="attend",
    )(seg_table, row_table, queries, bank)


def expert_rows(arrived, w_gate_up, w_down):
    shaped = arrived.shape
    flat_rows = arrived.reshape(-1, shaped[-1])
    projected = jnp.dot(flat_rows, w_gate_up[0], preferred_element_type=jnp.float32)
    hidden = (jax.nn.silu(projected[:, :FF]) * projected[:, FF:]).astype(jnp.bfloat16)
    produced = jnp.dot(hidden, w_down[0], preferred_element_type=jnp.float32).astype(jnp.bfloat16)
    return produced.reshape(shaped)


def on_device(
    resid,
    qkv,
    cache_kv,
    page_slot,
    seg_lengths,
    cache_age,
    w_out,
    norm_gain,
    routes,
    route_probs,
    w_gate_up,
    w_down,
):
    tok_groups = lax.axis_size("tok")
    ep_count = lax.axis_size("ep")
    member = lax.axis_index("ep")
    tok_dev = resid.shape[0]
    q_width = QPG * HEAD
    grouped = lax.all_to_all(qkv, "tok", split_axis=1, concat_axis=0, tiled=True)
    queries = grouped[:, :q_width]
    own_keys = grouped[:, q_width:]
    seg_count = seg_lengths.shape[0]
    page_count = cache_kv.shape[0]
    cached_rows = cache_kv.reshape(page_count * PAGE, 2 * HEAD)
    slots = jnp.broadcast_to(
        jnp.pad(page_slot, (0, 2 * HEAD - page_count))[None, :], (META_ROWS, 2 * HEAD)
    ).astype(jnp.bfloat16)
    own_bank = jnp.concatenate([own_keys, cached_rows, slots], axis=0)
    bank_rows = own_bank.shape[0]
    bank = lax.all_gather(own_bank, "ep", axis=0, tiled=True)
    held = bank.reshape(ep_count, bank_rows, 2 * HEAD)[:, bank_rows - 1, :page_count].astype(jnp.int32)
    first_cached = tok_groups * tok_dev
    slot_row = (
        jnp.arange(ep_count, dtype=jnp.int32)[:, None] * bank_rows
        + first_cached
        + jnp.arange(page_count, dtype=jnp.int32)[None, :] * PAGE
    )
    pages = seg_count * SEG_PAGES
    page_match = held.reshape(-1)[None, :] == jnp.arange(pages, dtype=jnp.int32)[:, None]
    page_row = jnp.sum(jnp.where(page_match, slot_row.reshape(-1)[None, :], 0), axis=1)
    chunk = jnp.arange(tok_groups * ep_count, dtype=jnp.int32)
    chunk_row = chunk % ep_count * bank_rows + chunk // ep_count * tok_dev
    row_table = jnp.concatenate([page_row, chunk_row]).astype(jnp.int32)
    seg_ends = jnp.cumsum(seg_lengths)
    first_tokens = (jnp.arange(tok_groups, dtype=jnp.int32) * ep_count + member) * tok_dev
    seg_table = jnp.concatenate([seg_ends - seg_lengths, seg_ends, cache_age, first_tokens]).astype(jnp.int32)
    attended = attention(
        seg_table, row_table, queries.reshape(tok_groups, tok_dev, q_width), bank, seg_count, SEG_MOST
    ).reshape(tok_groups * tok_dev, q_width)
    attn_sum = lax.psum_scatter(
        jnp.dot(attended, w_out, preferred_element_type=jnp.float32).astype(jnp.bfloat16),
        "tok",
        scatter_dimension=0,
        tiled=True,
    ).astype(jnp.float32)
    mixed = (resid.astype(jnp.float32) + attn_sum).astype(jnp.bfloat16)
    widened_mix = mixed.astype(jnp.float32)
    normed = (
        widened_mix
        * lax.rsqrt(jnp.mean(widened_mix * widened_mix, axis=-1, keepdims=True) + NORM_EPS)
        * norm_gain[None, :]
    ).astype(jnp.bfloat16)
    expert_count = tok_groups * ep_count
    capacity = max(2, 2 * tok_dev * TOP // expert_count)
    flat_route = routes.reshape(-1)
    one_hot = (flat_route[:, None] == jnp.arange(expert_count, dtype=jnp.int32)[None, :]).astype(
        jnp.int32
    )
    earlier = jnp.cumsum(one_hot, axis=0) - one_hot
    slot_rank = jnp.sum(earlier * one_hot, axis=1)
    slot_index = flat_route * capacity + slot_rank
    source_row = (
        jnp.full((expert_count * capacity,), tok_dev, jnp.int32)
        .at[slot_index]
        .set(jnp.arange(tok_dev * TOP, dtype=jnp.int32) // TOP)
    )
    padded = jnp.concatenate([normed, jnp.zeros((1, D), jnp.bfloat16)], axis=0)
    outgoing = padded[source_row].reshape(expert_count, capacity, D)
    returned = lax.all_to_all(
        expert_rows(
            lax.all_to_all(outgoing, ("tok", "ep"), split_axis=0, concat_axis=0, tiled=True),
            w_gate_up,
            w_down,
        ),
        ("tok", "ep"),
        split_axis=0,
        concat_axis=0,
        tiled=True,
    ).reshape(expert_count * capacity, D)
    picked = returned[slot_index].reshape(tok_dev, TOP, D)
    shares = route_probs / jnp.sum(route_probs, axis=1, keepdims=True)
    routed = jnp.einsum("tk,tkd->td", shares, picked, preferred_element_type=jnp.float32)
    return (widened_mix + routed).astype(jnp.bfloat16)


def solution(mesh):
    placed = (
        P(("tok", "ep"), None),
        P(("tok", "ep"), None),
        P("ep", "tok", None, None),
        P("ep"),
        P(),
        P(),
        P("tok", None),
        P(),
        P(("tok", "ep"), None),
        P(("tok", "ep"), None),
        P(("tok", "ep"), None, None),
        P(("tok", "ep"), None, None),
    )
    return jax.shard_map(
        on_device, mesh=mesh, in_specs=placed, out_specs=P(("tok", "ep"), None), check_vma=False
    )
```

time: 1260 us -> 450 us (0.36); the launches traced: 1230 us -> 443 us
  loops' own time: 261 us -> 0 us
  local copies, waits for them, and re-layouts: 241 us -> 46.6 us
  matrix products: 216 us -> 31.8 us
  other arithmetic: 116 us -> 10.9 us
  blocking collectives: 175 us -> 105 us
  Pallas kernels: 0 us -> 22.3 us
    another operation x385 -> x0, loops' own time: 261 us -> none  [the longest x1 253 us: on_device(): states, ignored = lax.scan(visit, states, blocks)]
    dot_general x102 -> x0, matrix products: 182 us -> none  [the longest x51 116 us: region_update(): jnp.dot(weights.astype(jnp.bfloat16), value_rows, preferred_element_type=...]
    reduce_or x96 -> x0, other arithmetic: 88.2 us -> none  [visit(): jnp.any(allowed)]
    squeeze x96 -> x0, local copies, waits for them, and re-layouts: 87.6 us -> none  [on_device(): states, ignored = lax.scan(visit, states, blocks)]
    reduce_scatter x1, waiting for transfers between devices: 99.6 us -> 27.7 us  [on_device(): lax.psum_scatter(jnp.dot(attended, w_out, preferred_element_type=jnp.floa...]
    dynamic_slice x96 -> x0, local copies, waits for them, and re-layouts: 68.1 us -> none  [on_device(): states, ignored = lax.scan(visit, states, blocks)]
    all_gather x1, waiting for transfers between devices: 8.66 us -> 59.6 us  [on_device(): bank = lax.all_gather(own_bank, 'ep', axis=0, tiled=True)]
    all_gather x2 -> x0, blocking collectives: 46.8 us -> none  [the longest x1 24.5 us: on_device(): piece_position = lax.all_gather(bank_position, 'ep', axis=0, tiled=True)]
  transfers between devices with their start and end apart: 3 -> 4, of which waited for: 3 -> 4; matrix products, arithmetic and copies ran while one was open for 1% -> 3% of each run, Pallas kernels for 0% -> 0%
where the time goes in v1:
time: 450 us; the launch traced here: 443 us
  waiting for transfers between devices  201 us (45%)
  blocking collectives  105 us (23%)
  local copies, waits for them, and re-layouts  46.6 us (10%)
  matrix products  31.8 us (7%)
  Pallas kernels  22.3 us (5%)
  between operations  13.7 us (3%)
  starting transfers between devices  12.1 us (3%)
  other arithmetic  10.9 us (2%)
    all_to_all x1, blocking collectives, on_device(): lax.all_to_all(outgoing, ('tok', 'ep'), split_axis=0, concat_axis=0, tile...  105 us
    all_to_all x1, waiting for transfers between devices, on_device(): lax.all_to_all(expert_rows(lax.all_to_all(outgoing, ('tok', 'ep'), split_...  95.9 us
    all_gather x1, waiting for transfers between devices, on_device(): bank = lax.all_gather(own_bank, 'ep', axis=0, tiled=True)  59.6 us
    reduce_scatter x1, waiting for transfers between devices, on_device(): lax.psum_scatter(jnp.dot(attended, w_out, preferred_element_type=jnp.floa...  27.7 us
    pallas_call x1, Pallas kernels, attention(): pl.pallas_call(functools.partial(attention_kernel, tok_dev, segs, most_st...  22.3 us
    gather x1, local copies, waits for them, and re-layouts, on_device(): outgoing = padded[source_row].reshape(expert_count, capacity, D)  17.5 us
    all_to_all x1, waiting for transfers between devices, on_device(): lax.all_to_all(qkv, 'tok', split_axis=1, concat_axis=0, tiled=True)  17.3 us
    dot_general x1, matrix products, expert_rows(): jnp.dot(flat_rows, w_gate_up[0], preferred_element_type=jnp.float32)  15.8 us
  transfers between devices with their start and end apart: 4, of which 4 were waited for; matrix products, arithmetic and copies ran while one was open for 3% of the time, Pallas kernels for 0%

profile of v1, /device:TPU:8, one launch (start us, length us, event | category | flops | bytes accessed | tf_op | source)
XLA Modules:
  0.0 442.7 jit_solution(758369617222762598)
XLA Ops:
  6.5 2.6 copy.39
  9.2 5.3 %all-to-all-start = ((bf16[128,4,1280]{2,0,1:T(8,128)(2,1)}), bf16[128,4,1280]{2,0,1:T(8,128)(2,1)}, u32[]{:S(2)}, u32[]{:S(2)}) async-start(bf16[128,4,1280]{2,0,1:T(8,128)(2,1)} %bitcast.53), calls=%async_computation | async-start | bytes 2621440 | tf_op jit(solution)/shard_map/all_to_all | solution.py:171
  14.5 0.7 convert.5
  15.1 17.3 %all-to-all-done = bf16[128,4,1280]{2,0,1:T(8,128)(2,1)} async-done(((bf16[128,4,1280]{2,0,1:T(8,128)(2,1)}), bf16[128,4,1280]{2,0,1:T(8,128)(2,1)}, u32[]{:S(2)}, u32[]{:S(2)}) %all-to-all-start) | async-done | bytes 1310752 | tf_op jit(solution)/shard_map/all_to_all | solution.py:171
  32.5 1.0 slice.32
  33.5 1.7 pad_maximum_fusion
  35.1 0.0 all-gather.2.cloned.1.call-update
  35.2 0.0 reduce-scatter.2.cloned.1.call-start
  35.2 0.1 broadcast_add_fusion.1
  35.3 0.1 add.109
  35.4 0.1 copy.24
  35.6 0.1 reduce
  35.7 0.1 pad_add_fusion.1.seg_ref
  35.8 2.3 slice.34
  38.1 59.6 %all-gather.2.cloned.1.call-done.bank_ref = bf16[25088,256]{1,0:T(8,128)(2,1)} async-done(((bf16[784,256]{1,0:T(8,128)(2,1)}), bf16[25088,256]{1,0:T(8,128)(2,1)}) %all-gather.2.cloned.1.call-update) | async-done | bytes 12845072 | tf_op jit(solution)/shard_map/all_gather | solution.py:182
  97.7 0.9 slice.33
  98.6 0.1 reshape.158
  98.7 0.1 select_reduce_fusion
  98.8 1.2 copy-done.1
  100.0 22.3 %attend.1 = bf16[4,128,1024]{2,1,0:T(8,128)(2,1)S(1)} custom-call(s32[52]{0:T(128)S(1)} %pad_add_fusion.1.seg_ref, s32[256]{0:T(256)S(1)} %pad_add_fusion.row_ref, bf16[4,128,1024]{2,1,0:T(8,128)(2,1)S(1)} %bitcast.47, bf16[25088,256]{1,0:T(8,128)(2,1)} %all-gather.2.cloned.1.call-done.bank_ref), custom_call_target="tpu_custom_call" | custom-call | tf_op jit(solution)/shard_map/attend/pallas_call | solution.py:126
  122.4 3.7 convolution_convert_fusion.1
  126.1 0.0 reduce-scatter.2.cloned.1.call-update
  126.2 0.1 copy.28
  126.3 0.1 eq.47
  126.4 0.1 eq.43
  126.4 0.1 copy.30
  126.5 0.2 fusion.14
  126.8 0.8 copy-done.2
  127.6 1.1 broadcast_add_fusion
  128.7 0.9 copy.31
  129.6 0.1 copy.27
  129.7 0.1 mul.98
  129.8 1.4 fusion.13
  131.2 4.3 scatter_custom_fusion
  135.5 27.7 %reduce-scatter.2.cloned.1.call-done = bf16[128,2048]{1,0:T(8,128)(2,1)} async-done(((bf16[512,2048]{1,0:T(8,128)(2,1)}), bf16[128,2048]{1,0:T(8,128)(2,1)}) %reduce-scatter.2.cloned.1.call-update) | async-done | bytes 524304 | tf_op jit(solution)/shard_map/reduce_scatter | solution.py:202
  163.2 1.5 fusion.8
  164.7 1.4 fusion.10
  166.1 0.9 concatenate.15
  167.0 17.5 %gather_fusion = bf16[2048,2048]{1,0:T(8,128)(2,1)} fusion(bf16[129,2048]{1,0:T(8,128)(2,1)} %concatenate.15, s32[2048]{0:T(1024)S(1)} %fusion.17), kind=kCustom, calls=%fused_computation | custom fusion | bytes 16785408 | tf_op jit(solution)/shard_map/gather | solution.py:230
  184.5 104.7 %all_to_all.29 = bf16[128,16,2048]{2,1,0:T(8,128)(2,1)S(1)} all-to-all(bf16[128,16,2048]{2,1,0:T(8,128)(2,1)} %bitcast.49), channel_id=1, replica_groups=mesh['tok'=4,'ep'=32] {'tok','ep'}, dimensions={0} | all-to-all | bytes 16777216 | tf_op jit(solution)/shard_map/all_to_all | solution.py:233
  289.1 15.8 %fusion.1 = f32[2048,1536]{1,0:T(8,128)S(1)} fusion(bf16[2048,2048]{1,0:T(8,128)(2,1)S(1)} %bitcast.52, bf16[1,2048,1536]{2,1,0:T(8,128)(2,1)} %param.22), kind=kOutput, calls=%fused_computation.6 | convolution fusion | flops 12884901888 | bytes 27262976 | tf_op jit(solution)/shard_map/dot_general | solution.py:146
  304.9 8.9 %convolution_convert_fusion = bf16[2048,2048]{1,0:T(8,128)(2,1)} fusion(f32[2048,1536]{1,0:T(8,128)S(1)} %fusion.1, bf16[1,768,2048]{2,1,0:T(8,128)(2,1)S(1)} %copy-done), kind=kOutput, calls=%fused_computation.3 | convolution fusion | flops 6456082432 | bytes 24117248 | tf_op jit(solution)/shard_map/dot_general | solution.py:148
  313.8 6.8 %all-to-all-start.2 = ((bf16[128,16,2048]{2,1,0:T(8,128)(2,1)}), bf16[128,16,2048]{2,1,0:T(8,128)(2,1)}, u32[]{:S(2)}, u32[]{:S(2)}) async-start(bf16[128,16,2048]{2,1,0:T(8,128)(2,1)} %bitcast.51), calls=%async_computation.3 | async-start | bytes 16777216 | tf_op jit(solution)/shard_map/all_to_all | solution.py:231
  320.7 0.1 copy.32
  320.8 95.9 %all-to-all-done.2 = bf16[128,16,2048]{2,1,0:T(8,128)(2,1)} async-done(((bf16[128,16,2048]{2,1,0:T(8,128)(2,1)}), bf16[128,16,2048]{2,1,0:T(8,128)(2,1)}, u32[]{:S(2)}, u32[]{:S(2)}) %all-to-all-start.2) | async-done | bytes 8388640 | tf_op jit(solution)/shard_map/all_to_all | solution.py:231
  416.7 13.3 %gather_fusion.1 = bf16[1024,2048]{1,0:T(8,128)(2,1)} fusion(bf16[2048,2048]{1,0:T(8,128)(2,1)} %bitcast.19, s32[1024]{0:T(1024)S(1)} %broadcast_clamp_fusion), kind=kCustom, calls=%fused_computation.1 | custom fusion | bytes 8392704 | tf_op jit(solution)/shard_map/gather | solution.py:242
  430.0 3.4 fusion.3
  433.4 2.4 fusion.11
  (38 shorter events, 0.2 us)
Async XLA Ops:
  6.5 298.4 %copy-start = (bf16[1,768,2048]{2,1,0:T(8,128)(2,1)S(1)}, bf16[1,768,2048]{2,1,0:T(8,128)(2,1)}, u32[]{:S(2)}) copy-start(bf16[1,768,2048]{2,1,0:T(8,128)(2,1)} %param.23) | copy-start | bytes 9437188
  6.5 28.9 %copy-start.6 = (s32[16]{0:T(128)S(1)}, s32[16]{0:T(128)}, u32[]{:S(2)}) copy-start(s32[16]{0:T(128)} %param.16) | copy-start | bytes 196
  6.5 29.2 %copy-start.7 = (s32[16]{0:T(128)S(1)}, s32[16]{0:T(128)}, u32[]{:S(2)}) copy-start(s32[16]{0:T(128)} %param.17) | copy-start | bytes 196
  9.2 23.3 %all-to-all-start = ((bf16[128,4,1280]{2,0,1:T(8,128)(2,1)}), bf16[128,4,1280]{2,0,1:T(8,128)(2,1)}, u32[]{:S(2)}, u32[]{:S(2)}) async-start(bf16[128,4,1280]{2,0,1:T(8,128)(2,1)} %bitcast.53), calls=%async_computation | async-start | bytes 2621440 | tf_op jit(solution)/shard_map/all_to_all | solution.py:171
  14.5 83.2 %all-gather.2.cloned.1.call-start = ((), (), s32[]{:S(2)}) async-start(), calls=%async_computation.4 | async-start | bytes 13246464 | tf_op jit(solution)/shard_map/all_gather | solution.py:182
  35.2 128.0 %reduce-scatter.2.cloned.1.call-start = ((), (), s32[]{:S(2)}) async-start(), calls=%async_computation.5 | async-start | bytes 2621440 | tf_op jit(solution)/shard_map/reduce_scatter | solution.py:202
  98.8 1.2 copy-start.1
  100.0 22.3 %copy-start.8 = (bf16[1024,2048]{1,0:T(8,128)(2,1)S(1)}, bf16[1024,2048]{1,0:T(8,128)(2,1)}, u32[]{:S(2)}) copy-start(bf16[1024,2048]{1,0:T(8,128)(2,1)} %param.18) | copy-start | bytes 12582916
  122.4 3.8 copy-start.3
  126.1 38.5 %copy-start.5 = (f32[2048]{0:T(1024)S(1)}, f32[2048]{0:T(1024)}, u32[]{:S(2)}) copy-start(f32[2048]{0:T(1024)} %param.19) | copy-start | bytes 24580
  126.8 0.8 copy-start.2
  313.8 6.8 %copy-start.4 = (f32[128,8]{0,1:T(8,128)S(1)}, f32[128,8]{0,1:T(8,128)}, u32[]{:S(2)}) copy-start(f32[128,8]{0,1:T(8,128)} %param.21) | copy-start | bytes 12292
  313.8 102.9 %all-to-all-start.2 = ((bf16[128,16,2048]{2,1,0:T(8,128)(2,1)}), bf16[128,16,2048]{2,1,0:T(8,128)(2,1)}, u32[]{:S(2)}, u32[]{:S(2)}) async-start(bf16[128,16,2048]{2,1,0:T(8,128)(2,1)} %bitcast.51), calls=%async_computation.3 | async-start | bytes 16777216 | tf_op jit(solution)/shard_map/all_to_all | solution.py:231
Sparse Core Ops, SparseCore 0:
  35.3 62.3 all-gather.1
  126.3 36.8 reduce-scatter.1

commit v2 on v1

--- a/solution.py
+++ b/solution.py
@@ -140,13 +140,205 @@
     )(seg_table, row_table, queries, bank)
 
 
-def expert_rows(arrived, w_gate_up, w_down):
-    shaped = arrived.shape
-    flat_rows = arrived.reshape(-1, shaped[-1])
-    projected = jnp.dot(flat_rows, w_gate_up[0], preferred_element_type=jnp.float32)
-    hidden = (jax.nn.silu(projected[:, :FF]) * projected[:, FF:]).astype(jnp.bfloat16)
-    produced = jnp.dot(hidden, w_down[0], preferred_element_type=jnp.float32).astype(jnp.bfloat16)
-    return produced.reshape(shaped)
+MESH = pl.DeviceIdType.MESH
+CAP = 16
+GROUP = 16
+MIX = 37
+
+def hop(dims, step, way):
+    deep, tall, wide, cores = dims
+    total = deep * tall * wide * cores
+    offset = lax.rem(step * MIX, total)
+    tok, ep = lax.axis_index("tok"), lax.axis_index("ep")
+    sizes = (deep, tall, wide, cores)
+    mine = (tok, lax.div(ep, wide * cores), lax.rem(lax.div(ep, cores), wide), lax.rem(ep, cores))
+    strides = (tall * wide * cores, wide * cores, cores, 1)
+    at = [
+        lax.rem(own + size + way * lax.rem(lax.div(offset, stride), size), size)
+        for own, size, stride in zip(mine, sizes, strides)
+    ]
+    place = (at[1] * wide + at[2]) * cores + at[3]
+    return (at[0], place), at[0] * (tall * wide * cores) + place
+
+
+def routed_kernel(
+    dims, normed_ref, mixed_ref, routes_ref, probs_ref, gate_up_hbm, down_hbm, out_ref,
+    stage, arrived, back, gate_up, down, rank, share, pick, total,
+    weight_sems, send_sems, recv_sems, back_send_sems, back_recv_sems,
+):
+    devices = dims[0] * dims[1] * dims[2] * dims[3]
+    chunks = devices // GROUP
+    rows = GROUP * CAP
+    tokens = normed_ref.shape[0]
+    hidden_width = down.shape[0]
+    load_gate_up = pltpu.make_async_copy(gate_up_hbm.at[0], gate_up, weight_sems.at[0])
+    load_down = pltpu.make_async_copy(down_hbm.at[0], down, weight_sems.at[1])
+    load_gate_up.start()
+    load_down.start()
+
+    barrier = pltpu.get_barrier_semaphore()
+
+    def greet(step, ignored):
+        pl.semaphore_signal(barrier, inc=1, device_id=hop(dims, step, 1)[0], device_id_type=MESH)
+        return ignored
+
+    lax.fori_loop(1, devices, greet, 0)
+
+    experts = lax.broadcasted_iota(jnp.int32, (devices, tokens), 0)
+    probs = probs_ref[...]
+    shares = probs / jnp.sum(probs, axis=0, keepdims=True)
+    named = jnp.zeros((devices, tokens), jnp.float32)
+    owed = jnp.zeros((devices, tokens), jnp.float32)
+    for k in range(routes_ref.shape[0]):
+        match = experts == routes_ref[k : k + 1, :]
+        named = jnp.where(match, 1.0, named)
+        owed = jnp.where(match, shares[k : k + 1, :], owed)
+    before = (
+        lax.broadcasted_iota(jnp.int32, (tokens, tokens), 0) < lax.broadcasted_iota(jnp.int32, (tokens, tokens), 1)
+    ).astype(jnp.bfloat16)
+    earlier = jnp.dot(named.astype(jnp.bfloat16), before, preferred_element_type=jnp.float32)
+    rank[...] = jnp.where(named > 0.0, earlier, -1.0)
+    share[...] = owed
+    slot = lax.broadcasted_iota(jnp.int32, (CAP, tokens), 0).astype(jnp.float32)
+
+    def slab(ref, step):
+        return ref.at[pl.ds(pl.multiple_of(step * CAP, CAP), CAP)]
+
+    def block(ref, chunk):
+        return ref.at[pl.ds(pl.multiple_of(chunk * rows, rows), rows)]
+
+    pl.semaphore_wait(barrier, devices - 1)
+
+    def dispatch(chunk, ignored):
+        def choose(j, inner):
+            expert = hop(dims, chunk * GROUP + j, 1)[1]
+            pick[pl.ds(pl.multiple_of(j * CAP, CAP), CAP), :] = jnp.where(
+                rank[pl.ds(expert, 1), :] == slot, 1.0, 0.0
+            ).astype(jnp.bfloat16)
+            return inner
+
+        lax.fori_loop(0, GROUP, choose, 0)
+        block(stage, chunk)[...] = jnp.dot(
+            pick[...], normed_ref[...], preferred_element_type=jnp.float32
+        ).astype(jnp.bfloat16)
+
+        def send(j, inner):
+            step = chunk * GROUP + j
+
+            @pl.when(step > 0)
+            def _():
+                pltpu.make_async_remote_copy(
+                    src_ref=slab(stage, step), dst_ref=slab(arrived, step),
+                    send_sem=send_sems.at[chunk], recv_sem=recv_sems.at[chunk],
+                    device_id=hop(dims, step, 1)[0], device_id_type=MESH,
+                ).start()
+
+            @pl.when(step == 0)
+            def _():
+                pltpu.make_async_copy(slab(stage, step), slab(arrived, step), recv_sems.at[chunk]).start()
+
+            return inner
+
+        return lax.fori_loop(0, GROUP, send, ignored)
+
+    lax.fori_loop(0, chunks, dispatch, 0)
+    load_gate_up.wait()
+    load_down.wait()
+
+    def work(chunk, ignored):
+        pltpu.make_async_copy(block(arrived, chunk), block(arrived, chunk), recv_sems.at[chunk]).wait()
+        came = block(arrived, chunk)[...]
+        gate = jnp.dot(came, gate_up[:, :hidden_width], preferred_element_type=jnp.float32)
+        up = jnp.dot(came, gate_up[:, hidden_width:], preferred_element_type=jnp.float32)
+        hidden = (gate * jax.nn.sigmoid(gate) * up).astype(jnp.bfloat16)
+        block(arrived, chunk)[...] = jnp.dot(hidden, down[...], preferred_element_type=jnp.float32).astype(jnp.bfloat16)
+
+        def give_back(j, inner):
+            step = chunk * GROUP + j
+
+            @pl.when(step > 0)
+            def _():
+                pltpu.make_async_remote_copy(
+                    src_ref=slab(arrived, step), dst_ref=slab(back, step),
+                    send_sem=back_send_sems.at[chunk], recv_sem=back_recv_sems.at[chunk],
+                    device_id=hop(dims, step, -1)[0], device_id_type=MESH,
+                ).start()
+
+            @pl.when(step == 0)
+            def _():
+                pltpu.make_async_copy(slab(arrived, step), slab(back, step), back_recv_sems.at[chunk]).start()
+
+            return inner
+
+        return lax.fori_loop(0, GROUP, give_back, ignored)
+
+    lax.fori_loop(0, chunks, work, 0)
+    total[...] = mixed_ref[...].astype(jnp.float32)
+
+    def combine(chunk, ignored):
+        def owe(j, inner):
+            expert = hop(dims, chunk * GROUP + j, 1)[1]
+            pick[pl.ds(pl.multiple_of(j * CAP, CAP), CAP), :] = jnp.where(
+                rank[pl.ds(expert, 1), :] == slot, share[pl.ds(expert, 1), :], 0.0
+            ).astype(jnp.bfloat16)
+            return inner
+
+        lax.fori_loop(0, GROUP, owe, 0)
+        pltpu.make_async_copy(block(back, chunk), block(back, chunk), back_recv_sems.at[chunk]).wait()
+        total[...] += lax.dot_general(
+            pick[...], block(back, chunk)[...], (((0,), (0,)), ((), ())), preferred_element_type=jnp.float32
+        )
+        return ignored
+
+    lax.fori_loop(0, chunks, combine, 0)
+    out_ref[...] = total[...].astype(jnp.bfloat16)
+
+    own = CAP
+    first = pl.ds(own, rows - own)
+    pltpu.make_async_copy(stage.at[first], stage.at[first], send_sems.at[0]).wait()
+    pltpu.make_async_copy(stage.at[first], stage.at[first], back_send_sems.at[0]).wait()
+
+    def settle(chunk, ignored):
+        pltpu.make_async_copy(block(stage, chunk), block(stage, chunk), send_sems.at[chunk]).wait()
+        pltpu.make_async_copy(block(stage, chunk), block(stage, chunk), back_send_sems.at[chunk]).wait()
+        return ignored
+
+    lax.fori_loop(1, chunks, settle, 0)
+
+
+def routed_experts(dims, normed, mixed, routes, probs, gate_up, down):
+    devices = dims[0] * dims[1] * dims[2] * dims[3]
+    chunks = devices // GROUP
+    tokens, width = normed.shape
+    slots = devices * CAP
+    vmem = pl.BlockSpec(memory_space=pltpu.VMEM)
+    kept = pl.BlockSpec(memory_space=pl.ANY)
+    flops = 2 * slots * width * (down.shape[1] * 3 + 2 * tokens)
+    return pl.pallas_call(
+        functools.partial(routed_kernel, dims),
+        out_shape=jax.ShapeDtypeStruct(mixed.shape, jnp.bfloat16),
+        in_specs=[vmem] * 4 + [kept] * 2,
+        out_specs=vmem,
+        scratch_shapes=[
+            pltpu.VMEM((slots, width), jnp.bfloat16),
+            pltpu.VMEM((slots, width), jnp.bfloat16),
+            pltpu.VMEM((slots, width), jnp.bfloat16),
+            pltpu.VMEM(gate_up.shape[1:], jnp.bfloat16),
+            pltpu.VMEM(down.shape[1:], jnp.bfloat16),
+            pltpu.VMEM((devices, tokens), jnp.float32),
+            pltpu.VMEM((devices, tokens), jnp.float32),
+            pltpu.VMEM((GROUP * CAP, tokens), jnp.bfloat16),
+            pltpu.VMEM((tokens, width), jnp.float32),
+            pltpu.SemaphoreType.DMA((2,)),
+            pltpu.SemaphoreType.DMA((chunks,)),
+            pltpu.SemaphoreType.DMA((chunks,)),
+            pltpu.SemaphoreType.DMA((chunks,)),
+            pltpu.SemaphoreType.DMA((chunks,)),
+        ],
+        compiler_params=pltpu.CompilerParams(collective_id=0, has_side_effects=True, vmem_limit_bytes=56 << 20),
+        cost_estimate=pl.CostEstimate(flops=flops, bytes_accessed=6 * slots * width * 2, transcendentals=0),
+        name="routed_experts",
+    )(normed, mixed, routes.T, probs.T, gate_up, down)
 
 
 def on_device(
@@ -212,37 +404,8 @@
         * lax.rsqrt(jnp.mean(widened_mix * widened_mix, axis=-1, keepdims=True) + NORM_EPS)
         * norm_gain[None, :]
     ).astype(jnp.bfloat16)
-    expert_count = tok_groups * ep_count
-    capacity = max(2, 2 * tok_dev * TOP // expert_count)
-    flat_route = routes.reshape(-1)
-    one_hot = (flat_route[:, None] == jnp.arange(expert_count, dtype=jnp.int32)[None, :]).astype(
-        jnp.int32
-    )
-    earlier = jnp.cumsum(one_hot, axis=0) - one_hot
-    slot_rank = jnp.sum(earlier * one_hot, axis=1)
-    slot_index = flat_route * capacity + slot_rank
-    source_row = (
-        jnp.full((expert_count * capacity,), tok_dev, jnp.int32)
-        .at[slot_index]
-        .set(jnp.arange(tok_dev * TOP, dtype=jnp.int32) // TOP)
-    )
-    padded = jnp.concatenate([normed, jnp.zeros((1, D), jnp.bfloat16)], axis=0)
-    outgoing = padded[source_row].reshape(expert_count, capacity, D)
-    returned = lax.all_to_all(
-        expert_rows(
-            lax.all_to_all(outgoing, ("tok", "ep"), split_axis=0, concat_axis=0, tiled=True),
-            w_gate_up,
-            w_down,
-        ),
-        ("tok", "ep"),
-        split_axis=0,
-        concat_axis=0,
-        tiled=True,
-    ).reshape(expert_count * capacity, D)
-    picked = returned[slot_index].reshape(tok_dev, TOP, D)
-    shares = route_probs / jnp.sum(route_probs, axis=1, keepdims=True)
-    routed = jnp.einsum("tk,tkd->td", shares, picked, preferred_element_type=jnp.float32)
-    return (widened_mix + routed).astype(jnp.bfloat16)
+    dims = (tok_groups, ep_count // 8, 4, 2)
+    return routed_experts(dims, normed, mixed, routes, route_probs, w_gate_up, w_down)
 
 
 def solution(mesh):

time: 450 us -> 412 us (0.916); the launches traced: 443 us -> 412 us
  Pallas kernels: 22.3 us -> 265 us
  blocking collectives: 105 us -> 0 us
  waiting for transfers between devices: 201 us -> 114 us
  local copies, waits for them, and re-layouts: 46.6 us -> 5.72 us
  matrix products: 31.8 us -> 3.71 us
  other arithmetic: 10.9 us -> 3.54 us
  starting transfers between devices: 12.1 us -> 5.35 us
    pallas_call x0 -> x1, Pallas kernels: none -> 238 us  [routed_experts(): pl.pallas_call(functools.partial(routed_kernel, dims), out_shape=jax.Shap...]
    all_to_all x1 -> x0, blocking collectives: 105 us -> none  [on_device(): lax.all_to_all(outgoing, ('tok', 'ep'), split_axis=0, concat_axis=0, tile...]
    all_to_all x1 -> x0, waiting for transfers between devices: 95.9 us -> none  [on_device(): lax.all_to_all(expert_rows(lax.all_to_all(outgoing, ('tok', 'ep'), split_...]
    gather x2 -> x0, local copies, waits for them, and re-layouts: 30.7 us -> none  [the longest x1 17.5 us: on_device(): outgoing = padded[source_row].reshape(expert_count, capacity, D)]
    dot_general x3 -> x0, matrix products: 28.1 us -> none  [the longest x1 15.8 us: expert_rows(): jnp.dot(flat_rows, w_gate_up[0], preferred_element_type=jnp.float32)]
    reduce_scatter x1, waiting for transfers between devices: 27.7 us -> 34.7 us  [on_device(): lax.psum_scatter(jnp.dot(attended, w_out, preferred_element_type=jnp.floa...]
    all_to_all x1 -> x0, starting transfers between devices: 6.78 us -> none  [on_device(): lax.all_to_all(expert_rows(lax.all_to_all(outgoing, ('tok', 'ep'), split_...]
    pallas_call x1, Pallas kernels: 22.3 us -> 27.1 us  [attention(): pl.pallas_call(functools.partial(attention_kernel, tok_dev, segs, most_st...]
  transfers between devices with their start and end apart: 4 -> 3, of which waited for: 4 -> 3; matrix products, arithmetic and copies ran while one was open for 3% -> 0% of each run, Pallas kernels for 0% -> 0%
where the time goes in v2:
time: 412 us
  Pallas kernels  265 us (64%)
  waiting for transfers between devices  114 us (28%)
  between operations  13.6 us (3%)
  local copies, waits for them, and re-layouts  5.72 us (1%)
  starting transfers between devices  5.35 us (1%)
    pallas_call x1, Pallas kernels, routed_experts(): pl.pallas_call(functools.partial(routed_kernel, dims), out_shape=jax.Shap...  238 us
    all_gather x1, waiting for transfers between devices, on_device(): bank = lax.all_gather(own_bank, 'ep', axis=0, tiled=True)  61.8 us
    reduce_scatter x1, waiting for transfers between devices, on_device(): lax.psum_scatter(jnp.dot(attended, w_out, preferred_element_type=jnp.floa...  34.7 us
    pallas_call x1, Pallas kernels, attention(): pl.pallas_call(functools.partial(attention_kernel, tok_dev, segs, most_st...  27.1 us
    all_to_all x1, waiting for transfers between devices, on_device(): lax.all_to_all(qkv, 'tok', split_axis=1, concat_axis=0, tiled=True)  17.9 us
  transfers between devices with their start and end apart: 3, of which 3 were waited for; matrix products, arithmetic and copies ran while one was open for 0% of the time, Pallas kernels for 0%

profile of v2, /device:TPU:8, one launch (start us, length us, event | category | flops | bytes accessed | tf_op | source)
XLA Modules:
  0.0 411.7 jit_solution(8583289519214163959)
XLA Ops:
  6.5 0.0 copy-start.7
  6.5 0.0 copy-start.2
  6.5 0.0 copy-start.4
  6.5 0.0 copy-start.5
  6.5 2.5 copy.26
  9.0 5.3 %all-to-all-start = ((bf16[128,4,1280]{2,0,1:T(8,128)(2,1)}), bf16[128,4,1280]{2,0,1:T(8,128)(2,1)S(1)}, u32[]{:S(2)}, u32[]{:S(2)}) async-start(bf16[128,4,1280]{2,0,1:T(8,128)(2,1)} %bitcast.17), calls=%async_computation | async-start | bytes 2621440 | tf_op jit(solution)/shard_map/all_to_all | solution.py:363
  14.3 0.0 all-gather.2.cloned.1.call-start
  14.4 0.0 copy-done.7
  14.4 17.9 %all-to-all-done = bf16[128,4,1280]{2,0,1:T(8,128)(2,1)S(1)} async-done(((bf16[128,4,1280]{2,0,1:T(8,128)(2,1)}), bf16[128,4,1280]{2,0,1:T(8,128)(2,1)S(1)}, u32[]{:S(2)}, u32[]{:S(2)}) %all-to-all-start) | async-done | bytes 1310752 | tf_op jit(solution)/shard_map/all_to_all | solution.py:363
  32.3 0.0 copy-done.2
  32.3 0.8 pad_maximum_fusion
  33.1 0.0 all-gather.2.cloned.1.call-update
  33.1 0.0 reduce-scatter.2.cloned.1.call-start
  33.1 0.0 copy-done.4
  33.2 0.1 copy.19
  33.3 0.1 reduce
  33.4 0.1 broadcast_add_fusion
  33.5 0.1 add.72
  33.6 0.0 copy-done.5
  33.6 0.1 pad_add_fusion.1.seg_ref
  33.7 0.1 slice.14
  33.9 61.8 %all-gather.2.cloned.1.call-done.bank_ref = bf16[25088,256]{1,0:T(8,128)(2,1)} async-done(((bf16[784,256]{1,0:T(8,128)(2,1)}), bf16[25088,256]{1,0:T(8,128)(2,1)}) %all-gather.2.cloned.1.call-update) | async-done | bytes 12845072 | tf_op jit(solution)/shard_map/all_gather | solution.py:374
  95.6 0.9 slice.13
  96.5 0.1 reshape.90
  96.6 0.1 select_reduce_fusion
  96.7 0.0 copy-start.6
  96.7 27.1 %attend.1 = bf16[4,128,1024]{2,1,0:T(8,128)(2,1)S(1)} custom-call(s32[52]{0:T(128)S(1)} %pad_add_fusion.1.seg_ref, s32[256]{0:T(256)S(1)} %pad_add_fusion.row_ref, bf16[4,128,1024]{2,1,0:T(8,128)(2,1)S(1)} %bitcast.18, bf16[25088,256]{1,0:T(8,128)(2,1)} %all-gather.2.cloned.1.call-done.bank_ref), custom_call_target="tpu_custom_call" | custom-call | tf_op jit(solution)/shard_map/attend/pallas_call | solution.py:126
  123.9 0.0 copy-done.6
  123.9 0.0 copy-start.1
  123.9 0.0 copy-start.3
  123.9 3.7 convolution_convert_fusion
  127.6 0.0 reduce-scatter.2.cloned.1.call-update
  127.6 34.7 %reduce-scatter.2.cloned.1.call-done = bf16[128,2048]{1,0:T(8,128)(2,1)} async-done(((bf16[512,2048]{1,0:T(8,128)(2,1)}), bf16[128,2048]{1,0:T(8,128)(2,1)}) %reduce-scatter.2.cloned.1.call-update) | async-done | bytes 524304 | tf_op jit(solution)/shard_map/reduce_scatter | solution.py:394
  162.3 0.0 copy-done.1
  162.3 1.3 fusion
  163.6 0.0 copy-start
  163.6 0.0 copy-done.3
  163.6 1.0 fusion.2.normed_ref
  164.6 0.0 copy-done
  164.6 238.3 %routed_experts.1 = bf16[128,2048]{1,0:T(8,128)(2,1)} custom-call(bf16[128,2048]{1,0:T(8,128)(2,1)} %fusion.2.normed_ref, bf16[128,2048]{1,0:T(8,128)(2,1)} %copy-done, s32[8,128]{1,0:T(8,128)} %bitcast.26, f32[8,128]{1,0:T(8,128)} %bitcast.27, bf16[1,2048,1536]{2,1,0:T(8,128)(2,1)} %gate_up_hbm.1, bf16[1,768,2048]{2,1,0:T(8,128)(2,1)} %down_hbm.1), custom_call_target="tpu_custom_call" | custom-call | flops 21474836480 | bytes 50331648 | tf_op jit(solution)/shard_map/routed_experts/pallas_call | solution.py:317
  402.9 1.9 copy.28
  (13 shorter events, 0.1 us)
Async XLA Ops:
  6.5 7.8 %copy-start.7 = (s32[4]{0:T(128)S(1)}, s32[4]{0:T(128)}, u32[]{:S(2)}) copy-start(s32[4]{0:T(128)} %param.15) | copy-start | bytes 52
  6.5 25.8 %copy-start.2 = (bf16[4,1,64,256]{3,2,1,0:T(8,128)(2,1)S(1)}, bf16[4,1,64,256]{3,2,1,0:T(8,128)(2,1)}, u32[]{:S(2)}) copy-start(bf16[4,1,64,256]{3,2,1,0:T(8,128)(2,1)} %param.14) | copy-start | bytes 393220
  6.5 26.6 %copy-start.4 = (s32[16]{0:T(128)S(1)}, s32[16]{0:T(128)}, u32[]{:S(2)}) copy-start(s32[16]{0:T(128)} %param.16) | copy-start | bytes 196
  6.5 27.1 %copy-start.5 = (s32[16]{0:T(128)S(1)}, s32[16]{0:T(128)}, u32[]{:S(2)}) copy-start(s32[16]{0:T(128)} %param.17) | copy-start | bytes 196
  9.0 23.2 %all-to-all-start = ((bf16[128,4,1280]{2,0,1:T(8,128)(2,1)}), bf16[128,4,1280]{2,0,1:T(8,128)(2,1)S(1)}, u32[]{:S(2)}, u32[]{:S(2)}) async-start(bf16[128,4,1280]{2,0,1:T(8,128)(2,1)} %bitcast.17), calls=%async_computation | async-start | bytes 2621440 | tf_op jit(solution)/shard_map/all_to_all | solution.py:363
  14.3 81.3 %all-gather.2.cloned.1.call-start = ((), (), s32[]{:S(2)}) async-start(), calls=%async_computation.2 | async-start | bytes 13246464 | tf_op jit(solution)/shard_map/all_gather | solution.py:374
  33.1 129.2 %reduce-scatter.2.cloned.1.call-start = ((), (), s32[]{:S(2)}) async-start(), calls=%async_computation.3 | async-start | bytes 2621440 | tf_op jit(solution)/shard_map/reduce_scatter | solution.py:394
  96.7 27.1 %copy-start.6 = (bf16[1024,2048]{1,0:T(8,128)(2,1)S(1)}, bf16[1024,2048]{1,0:T(8,128)(2,1)}, u32[]{:S(2)}) copy-start(bf16[1024,2048]{1,0:T(8,128)(2,1)} %param.18) | copy-start | bytes 12582916
  123.9 38.4 %copy-start.1 = (bf16[128,2048]{1,0:T(8,128)(2,1)S(1)}, bf16[128,2048]{1,0:T(8,128)(2,1)}, u32[]{:S(2)}) copy-start(bf16[128,2048]{1,0:T(8,128)(2,1)} %param.12) | copy-start | bytes 1572868
  123.9 39.7 %copy-start.3 = (f32[2048]{0:T(1024)S(1)}, f32[2048]{0:T(1024)}, u32[]{:S(2)}) copy-start(f32[2048]{0:T(1024)} %param.19) | copy-start | bytes 24580
  163.6 1.0 copy-start
Sparse Core Ops, SparseCore 0:
  33.2 62.3 all-gather.1
  127.8 34.4 reduce-scatter.1

commit v3 on v2

--- a/solution.py
+++ b/solution.py
@@ -24,9 +24,10 @@
 NORM_EPS = 1e-06
 
 
-def attention_kernel(tok_dev, segs, most_steps, seg_ref, row_ref, q_ref, bank_ref, out_ref, score_ref, low_ref, top_ref, den_ref, acc_ref):
+def attention_kernel(tok_dev, segs, most_steps, seg_ref, row_ref, q_ref, window_ref, bank_ref, out_ref, score_ref, low_ref, top_ref, den_ref, acc_ref):
     rows = tok_dev * QPG
-    pages = segs * SEG_PAGES
+    held_chunks = window_ref.shape[0] // tok_dev
+    opening_chunk = seg_ref[3 * segs] // tok_dev - (held_chunks - q_ref.shape[0])
     rate = math.log2(math.e) / math.sqrt(HEAD)
 
     def tiled(mask):
@@ -48,14 +49,14 @@
         den_ref[...] = jnp.zeros_like(den_ref)
         acc_ref[...] = jnp.zeros_like(acc_ref)
 
-        def region(steps, bank_of, mask_of, opening):
+        def region(bank, steps, bank_of, mask_of, opening):
             if opening:
                 held = jnp.full((rows, HEAD), NEG_FILL, jnp.float32)
             else:
                 held = top_ref[...]
 
             def score(step, running):
-                keys = jnp.concatenate([bank_ref[pl.ds(at, size), :HEAD] for at, size in bank_of(step)], axis=0)
+                keys = jnp.concatenate([bank[pl.ds(at, size), :HEAD] for at, size in bank_of(step)], axis=0)
                 scores = lax.dot_general(query, keys, (((1,), (1,)), ((), ())), preferred_element_type=jnp.float32) * rate
                 scores = jnp.where(tiled(mask_of(step)), scores, NEG_FILL)
                 score_ref[step] = scores
@@ -73,7 +74,7 @@
                 top = top_ref[...]
                 weights = jnp.exp2(score_ref[step] - jnp.concatenate([top, top], axis=1))
                 den_ref[...] += weights[:, :HEAD] + weights[:, HEAD:]
-                values = jnp.concatenate([bank_ref[pl.ds(at, size), HEAD:] for at, size in bank_of(step)], axis=0)
+                values = jnp.concatenate([bank[pl.ds(at, size), HEAD:] for at, size in bank_of(step)], axis=0)
                 acc_ref[...] += jnp.dot(weights.astype(jnp.bfloat16), values, preferred_element_type=jnp.float32)
                 return ignored
 
@@ -87,13 +88,16 @@
             return chunk_last - 2 * step - 1 + half
 
         def new_bank(step):
-            return [(pl.multiple_of(row_ref[pages + jnp.maximum(new_chunk(step, half), 0)], 16), tok_dev) for half in range(2)]
+            return [
+                (pl.multiple_of(jnp.clip(new_chunk(step, half) - opening_chunk, 0, held_chunks - 1) * tok_dev, tok_dev), tok_dev)
+                for half in range(2)
+            ]
 
         def new_mask(step):
             key = new_chunk(step, 0) * tok_dev + column
             return (key >= low_ref[...]) & (key <= token)
 
-        region(steps, new_bank, new_mask, True)
+        region(window_ref, steps, new_bank, new_mask, True)
 
         def cached(s, ignored):
             start, end, age = seg_ref[s], seg_ref[segs + s], seg_ref[2 * segs + s]
@@ -106,7 +110,7 @@
                 def page_mask(step):
                     return (token >= start) & (token < end) & (step * STEP + column < age)
 
-                region((age + STEP - 1) // STEP, page_bank, page_mask, False)
+                region(bank_ref, (age + STEP - 1) // STEP, page_bank, page_mask, False)
             return ignored
 
         lax.fori_loop(0, segs, cached, 0)
@@ -119,14 +123,14 @@
     lax.fori_loop(0, q_ref.shape[0], one_block, 0)
 
 
-def attention(seg_table, row_table, queries, bank, segs, seg_most):
+def attention(seg_table, row_table, queries, window, bank, segs, seg_most):
     blocks, tok_dev, width = queries.shape
     most_steps = max((seg_most + tok_dev) // tok_dev // 2 + 1, SEG_PAGES * PAGE // STEP)
     rows = tok_dev * QPG
     return pl.pallas_call(
         functools.partial(attention_kernel, tok_dev, segs, most_steps),
         out_shape=jax.ShapeDtypeStruct(queries.shape, jnp.bfloat16),
-        in_specs=[pl.BlockSpec(memory_space=pltpu.SMEM)] * 2 + [pl.BlockSpec(memory_space=pltpu.VMEM)] * 2,
+        in_specs=[pl.BlockSpec(memory_space=pltpu.SMEM)] * 2 + [pl.BlockSpec(memory_space=pltpu.VMEM)] * 3,
         out_specs=pl.BlockSpec(memory_space=pltpu.VMEM),
         scratch_shapes=[
             pltpu.VMEM((most_steps, rows, STEP), jnp.float32),
@@ -137,10 +141,302 @@
         ],
         compiler_params=pltpu.CompilerParams(vmem_limit_bytes=48 << 20),
         name="attend",
-    )(seg_table, row_table, queries, bank)
+    )(seg_table, row_table, queries, window, bank)
 
 
 MESH = pl.DeviceIdType.MESH
+
+
+def place_of(group, head):
+    tok, tall, core = lax.div(group, 8), lax.rem(lax.div(group, 2), 4), lax.rem(group, 2)
+    return (tall * 4 + lax.rem(tok + head, 4)) * 2 + core
+
+
+def group_at(ep, head):
+    tall, wide, core = lax.div(ep, 8), lax.rem(lax.div(ep, 2), 4), lax.rem(ep, 2)
+    return lax.rem(wide + 4 - head, 4) * 8 + 2 * tall + core
+
+
+def owner_of(group, block):
+    tok = lax.div(group, 8)
+    return tok, lax.rem(group, 8) * 4 + block
+
+
+def exchange_kernel(
+    qkv_ref, cache_ref, slots_ref, query_ref, window_ref, bank_ref,
+    stage_q, stage_kv, load_sems, key_send, key_recv, query_send, query_recv, pass_send, pass_recv, own_sem, line_send, line_recv,
+    plane_send, plane_recv, pair_send, pair_recv,
+):
+    tok, ep = lax.axis_index("tok"), lax.axis_index("ep")
+    tok_dev = qkv_ref.shape[0]
+    q_width = QPG * HEAD
+    number = tok * 32 + ep
+    group, block = lax.div(number, 4), lax.rem(number, 4)
+    mine = group_at(ep, tok)
+    reach = SEG_MOST // (4 * tok_dev)
+    span = 4 * tok_dev
+
+    def column(head):
+        return head * (q_width + 2 * HEAD)
+
+    def remote(source, place, send_sem, recv_sem, device):
+        return pltpu.make_async_remote_copy(
+            src_ref=source, dst_ref=place, send_sem=send_sem, recv_sem=recv_sem, device_id=device, device_id_type=MESH
+        )
+
+    def load(turn, keys):
+        head = lax.rem(tok + turn, 4)
+        if keys:
+            source = qkv_ref.at[:, pl.ds(pl.multiple_of(column(head) + q_width, HEAD), 2 * HEAD)]
+            return pltpu.make_async_copy(source, stage_kv.at[turn], load_sems.at[turn])
+        source = qkv_ref.at[:, pl.ds(pl.multiple_of(column(head), HEAD), q_width)]
+        return pltpu.make_async_copy(source, stage_q.at[turn], load_sems.at[4 + turn])
+
+    for keys in (True, False):
+        for turn in range(4):
+            load(turn, keys).start()
+
+    def key_copy(turn):
+        head = lax.rem(tok + turn, 4)
+        place = window_ref.at[pl.ds(pl.multiple_of(reach * span + block * tok_dev, tok_dev), tok_dev)]
+        return stage_kv.at[turn], place, key_send.at[turn], key_recv, (head, place_of(group, head))
+
+    def query_copy(turn):
+        head = lax.rem(tok + turn, 4)
+        return stage_q.at[turn], query_ref.at[block], query_send.at[turn], query_recv, (head, place_of(group, head))
+
+    def spans(index):
+        return window_ref.at[pl.ds(pl.multiple_of(index * span, span), span)]
+
+    def pass_copy(turn):
+        device = (tok, place_of(lax.rem(mine + 2 * turn, 32), tok))
+        return spans(reach), spans(reach - 2 * turn), pass_send.at[turn - 1], pass_recv.at[turn - 1], device
+
+    def cross_copy(turn):
+        device = (tok, at(tall, wide, 1 - core))
+        return spans(6 - 2 * turn - 2 * core), spans(5 - 2 * turn), pass_send.at[turn + 1], pass_recv.at[turn + 1], device
+
+    held, told = cache_ref.shape[0], slots_ref.shape[0]
+    piece = held + told
+    cut = piece // 32 * 16
+    tall, wide, core = lax.div(ep, 8), lax.rem(lax.div(ep, 2), 4), lax.rem(ep, 2)
+
+    def at(y, x, c):
+        return (lax.rem(y, 4) * 4 + lax.rem(x, 4)) * 2 + c
+
+    def part(y, x, c, start, size):
+        return bank_ref.at[pl.ds(pl.multiple_of(at(y, x, c) * piece + start, 16), size)]
+
+    own_cache = pltpu.make_async_copy(cache_ref, part(tall, wide, core, 0, held), own_sem.at[0])
+    own_slots = pltpu.make_async_copy(slots_ref, part(tall, wide, core, held, told), own_sem.at[1])
+    own_cache.start()
+    own_slots.start()
+
+    def line_copies():
+        for turn in range(1, 4):
+            first = part(tall, wide, core, 0, cut)
+            yield remote(first, first, line_send, line_recv, (tok, at(tall, wide + turn, core)))
+            rest = part(tall, wide, core, cut, piece - cut)
+            yield remote(rest, rest, line_send, line_recv, (tok, at(tall + turn, wide, core)))
+
+    def plane_copies():
+        for turn in range(1, 4):
+            for along in range(4):
+                first = part(tall, wide + along, core, 0, cut)
+                yield remote(first, first, plane_send, plane_recv, (tok, at(tall + turn, wide, core)))
+                rest = part(tall + along, wide, core, cut, piece - cut)
+                yield remote(rest, rest, plane_send, plane_recv, (tok, at(tall, wide + turn, core)))
+
+    def pair_copies():
+        for y in range(4):
+            for x in range(4):
+                whole = part(y, x, core, 0, piece)
+                yield remote(whole, whole, pair_send, pair_recv, (tok, at(tall, wide, 1 - core)))
+
+    def settle(rows, sem):
+        pltpu.make_async_copy(bank_ref.at[pl.ds(0, rows)], bank_ref.at[pl.ds(0, rows)], sem).wait()
+
+    barrier = pltpu.get_barrier_semaphore()
+    at_home = place_of(group, tok) == ep
+    for turn in range(1, 4):
+        for partner in (at(tall, wide + turn, core), at(tall + turn, wide, core)):
+            pl.semaphore_signal(barrier, inc=1, device_id=(tok, partner), device_id_type=MESH)
+    pl.semaphore_signal(barrier, inc=1, device_id=(tok, at(tall, wide, 1 - core)), device_id_type=MESH)
+    for turn in range(4):
+        theirs = owner_of(mine, turn)
+
+        @pl.when(jnp.logical_not((theirs[0] == tok) & (theirs[1] == ep)))
+        def _():
+            pl.semaphore_signal(barrier, inc=1, device_id=theirs, device_id_type=MESH)
+
+    for turn in range(1, 3):
+        pl.semaphore_signal(
+            barrier, inc=1, device_id=(tok, place_of(lax.rem(mine + 32 - 2 * turn, 32), tok)), device_id_type=MESH
+        )
+    pl.semaphore_wait(barrier, 13 - jnp.where(at_home, 1, 0))
+
+    own_cache.wait()
+    own_slots.wait()
+    for copy in (key_copy, query_copy):
+        if copy is query_copy:
+            for line_copy in line_copies():
+                line_copy.start()
+        for turn in range(4):
+            source, place, send_sem, recv_sem, device = copy(turn)
+            load(turn, copy is key_copy).wait()
+            if turn == 0:
+
+                @pl.when(at_home)
+                def _():
+                    pltpu.make_async_copy(source, place, recv_sem).start()
+
+                @pl.when(jnp.logical_not(at_home))
+                def _():
+                    remote(source, place, send_sem, recv_sem, device).start()
+            else:
+                remote(source, place, send_sem, recv_sem, device).start()
+    own = window_ref.at[pl.ds(reach * span, span)]
+    pltpu.make_async_copy(own, own, key_recv).wait()
+    for turn in range(1, 3):
+        remote(*pass_copy(turn)).start()
+    settle(3 * piece, line_recv)
+    for plane_copy in plane_copies():
+        plane_copy.start()
+    settle(12 * piece, plane_recv)
+    for pair_copy in pair_copies():
+        pair_copy.start()
+    for turn in range(1, 3):
+        remote(*pass_copy(turn)).wait()
+    for turn in range(1, 3):
+        remote(*cross_copy(turn)).start()
+    for turn in range(1, 3):
+        remote(*cross_copy(turn)).wait()
+    pltpu.make_async_copy(query_ref, query_ref, query_recv).wait()
+    for copy in (key_copy, query_copy):
+        for turn in range(4):
+            if turn == 0:
+
+                @pl.when(jnp.logical_not(at_home))
+                def _():
+                    remote(*copy(turn)).wait_send()
+            else:
+                remote(*copy(turn)).wait_send()
+    settle(16 * piece, pair_recv)
+    settle(3 * piece, line_send)
+    settle(12 * piece, plane_send)
+    settle(16 * piece, pair_send)
+
+
+def exchange(qkv, cached, slots):
+    tok_dev = qkv.shape[0]
+    reach = SEG_MOST // (4 * tok_dev)
+    kept = pl.BlockSpec(memory_space=pl.ANY)
+    return pl.pallas_call(
+        exchange_kernel,
+        out_shape=(
+            jax.ShapeDtypeStruct((4, tok_dev, QPG * HEAD), jnp.bfloat16),
+            jax.ShapeDtypeStruct(((reach + 1) * 4 * tok_dev, 2 * HEAD), jnp.bfloat16),
+            jax.ShapeDtypeStruct((32 * (cached.shape[0] + slots.shape[0]), 2 * HEAD), jnp.bfloat16),
+        ),
+        in_specs=[kept] * 3,
+        out_specs=(kept,) * 3,
+        scratch_shapes=[
+            pltpu.VMEM((4, tok_dev, QPG * HEAD), jnp.bfloat16),
+            pltpu.VMEM((4, tok_dev, 2 * HEAD), jnp.bfloat16),
+            pltpu.SemaphoreType.DMA((8,)),
+            pltpu.SemaphoreType.DMA((4,)),
+            pltpu.SemaphoreType.DMA,
+            pltpu.SemaphoreType.DMA((4,)),
+            pltpu.SemaphoreType.DMA,
+            pltpu.SemaphoreType.DMA((4,)),
+            pltpu.SemaphoreType.DMA((4,)),
+            pltpu.SemaphoreType.DMA((2,)),
+        ]
+        + [pltpu.SemaphoreType.DMA] * 6,
+        compiler_params=pltpu.CompilerParams(collective_id=1, has_side_effects=True),
+        cost_estimate=pl.CostEstimate(flops=0, bytes_accessed=80 << 20, transcendentals=0),
+        name="exchange",
+    )(qkv, cached, slots)
+
+
+def project_kernel(
+    attended_ref, weight_ref, resid_ref, gain_ref, mixed_ref, normed_ref, stage, inbox, send_sems, recv_sem
+):
+    tok, ep = lax.axis_index("tok"), lax.axis_index("ep")
+    blocks, tok_dev, width = attended_ref.shape
+    number = tok * 32 + ep
+    group = lax.div(number, 4)
+    mine = group_at(ep, tok)
+    barrier = pltpu.get_barrier_semaphore()
+    for turn in range(4):
+        head = lax.rem(tok + turn, 4)
+        target = place_of(group, head)
+
+        @pl.when(jnp.logical_not((target == ep) & (head == tok)))
+        def _():
+            pl.semaphore_signal(barrier, inc=1, device_id=(head, target), device_id_type=MESH)
+
+    home = [owner_of(mine, block) for block in range(blocks)]
+    is_own = [(place[0] == tok) & (place[1] == ep) for place in home]
+    others = 4 - sum([jnp.where(flag, 1, 0) for flag in is_own])
+    pl.semaphore_wait(barrier, others)
+
+    def copy(block):
+        return pltpu.make_async_remote_copy(
+            src_ref=stage.at[block], dst_ref=inbox.at[tok], send_sem=send_sems.at[block], recv_sem=recv_sem,
+            device_id=home[block], device_id_type=MESH,
+        )
+
+    for block in range(blocks):
+        stage[block] = jnp.dot(
+            attended_ref[block], weight_ref[...], preferred_element_type=jnp.float32
+        ).astype(jnp.bfloat16)
+
+        @pl.when(is_own[block])
+        def _():
+            pltpu.make_async_copy(stage.at[block], inbox.at[tok], recv_sem).start()
+
+        @pl.when(jnp.logical_not(is_own[block]))
+        def _():
+            copy(block).start()
+
+    pltpu.make_async_copy(inbox, inbox, recv_sem).wait()
+    added = resid_ref[...].astype(jnp.float32)
+    for head in range(4):
+        added = added + inbox[head].astype(jnp.float32)
+    mixed = added.astype(jnp.bfloat16)
+    mixed_ref[...] = mixed
+    wide = mixed.astype(jnp.float32)
+    level = lax.rsqrt(jnp.mean(wide * wide, axis=-1, keepdims=True) + NORM_EPS)
+    normed_ref[...] = (wide * level * gain_ref[...]).astype(jnp.bfloat16)
+    for block in range(blocks):
+
+        @pl.when(jnp.logical_not(is_own[block]))
+        def _():
+            copy(block).wait_send()
+
+
+def project(attended, weight, resid, gain):
+    blocks, tok_dev, width = attended.shape
+    out = weight.shape[1]
+    vmem = pl.BlockSpec(memory_space=pltpu.VMEM)
+    return pl.pallas_call(
+        project_kernel,
+        out_shape=(jax.ShapeDtypeStruct(resid.shape, jnp.bfloat16),) * 2,
+        in_specs=[vmem] * 4,
+        out_specs=(vmem, vmem),
+        scratch_shapes=[
+            pltpu.VMEM((blocks, tok_dev, out), jnp.bfloat16),
+            pltpu.VMEM((4, tok_dev, out), jnp.bfloat16),
+            pltpu.SemaphoreType.DMA((blocks,)),
+            pltpu.SemaphoreType.DMA,
+        ],
+        compiler_params=pltpu.CompilerParams(collective_id=2, has_side_effects=True, vmem_limit_bytes=40 << 20),
+        cost_estimate=pl.CostEstimate(flops=2 * blocks * tok_dev * width * out, bytes_accessed=40 << 20, transcendentals=0),
+        name="project",
+    )(attended, weight, resid, gain[None, :])
+
+
 CAP = 16
 GROUP = 16
 MIX = 37
@@ -357,53 +653,27 @@
 ):
     tok_groups = lax.axis_size("tok")
     ep_count = lax.axis_size("ep")
-    member = lax.axis_index("ep")
     tok_dev = resid.shape[0]
-    q_width = QPG * HEAD
-    grouped = lax.all_to_all(qkv, "tok", split_axis=1, concat_axis=0, tiled=True)
-    queries = grouped[:, :q_width]
-    own_keys = grouped[:, q_width:]
     seg_count = seg_lengths.shape[0]
     page_count = cache_kv.shape[0]
-    cached_rows = cache_kv.reshape(page_count * PAGE, 2 * HEAD)
     slots = jnp.broadcast_to(
         jnp.pad(page_slot, (0, 2 * HEAD - page_count))[None, :], (META_ROWS, 2 * HEAD)
     ).astype(jnp.bfloat16)
-    own_bank = jnp.concatenate([own_keys, cached_rows, slots], axis=0)
-    bank_rows = own_bank.shape[0]
-    bank = lax.all_gather(own_bank, "ep", axis=0, tiled=True)
+    bank_rows = page_count * PAGE + META_ROWS
+    queries, window, bank = exchange(qkv, cache_kv.reshape(page_count * PAGE, 2 * HEAD), slots)
     held = bank.reshape(ep_count, bank_rows, 2 * HEAD)[:, bank_rows - 1, :page_count].astype(jnp.int32)
-    first_cached = tok_groups * tok_dev
     slot_row = (
         jnp.arange(ep_count, dtype=jnp.int32)[:, None] * bank_rows
-        + first_cached
         + jnp.arange(page_count, dtype=jnp.int32)[None, :] * PAGE
     )
-    pages = seg_count * SEG_PAGES
-    page_match = held.reshape(-1)[None, :] == jnp.arange(pages, dtype=jnp.int32)[:, None]
-    page_row = jnp.sum(jnp.where(page_match, slot_row.reshape(-1)[None, :], 0), axis=1)
-    chunk = jnp.arange(tok_groups * ep_count, dtype=jnp.int32)
-    chunk_row = chunk % ep_count * bank_rows + chunk // ep_count * tok_dev
-    row_table = jnp.concatenate([page_row, chunk_row]).astype(jnp.int32)
+    page_match = held.reshape(-1)[None, :] == jnp.arange(seg_count * SEG_PAGES, dtype=jnp.int32)[:, None]
+    row_table = jnp.sum(jnp.where(page_match, slot_row.reshape(-1)[None, :], 0), axis=1).astype(jnp.int32)
     seg_ends = jnp.cumsum(seg_lengths)
-    first_tokens = (jnp.arange(tok_groups, dtype=jnp.int32) * ep_count + member) * tok_dev
+    blocks = queries.shape[0]
+    first_tokens = (group_at(lax.axis_index("ep"), lax.axis_index("tok")) * blocks + jnp.arange(blocks, dtype=jnp.int32)) * tok_dev
     seg_table = jnp.concatenate([seg_ends - seg_lengths, seg_ends, cache_age, first_tokens]).astype(jnp.int32)
-    attended = attention(
-        seg_table, row_table, queries.reshape(tok_groups, tok_dev, q_width), bank, seg_count, SEG_MOST
-    ).reshape(tok_groups * tok_dev, q_width)
-    attn_sum = lax.psum_scatter(
-        jnp.dot(attended, w_out, preferred_element_type=jnp.float32).astype(jnp.bfloat16),
-        "tok",
-        scatter_dimension=0,
-        tiled=True,
-    ).astype(jnp.float32)
-    mixed = (resid.astype(jnp.float32) + attn_sum).astype(jnp.bfloat16)
-    widened_mix = mixed.astype(jnp.float32)
-    normed = (
-        widened_mix
-        * lax.rsqrt(jnp.mean(widened_mix * widened_mix, axis=-1, keepdims=True) + NORM_EPS)
-        * norm_gain[None, :]
-    ).astype(jnp.bfloat16)
+    attended = attention(seg_table, row_table, queries, window, bank, seg_count, SEG_MOST)
+    mixed, normed = project(attended, w_out, resid, norm_gain)
     dims = (tok_groups, ep_count // 8, 4, 2)
     return routed_experts(dims, normed, mixed, routes, route_probs, w_gate_up, w_down)
 

time: 412 us -> 354 us (0.86); the launches traced: 412 us -> 347 us
  waiting for transfers between devices: 114 us -> 0 us
  Pallas kernels: 265 us -> 336 us
  between operations: 13.6 us -> 0.12 us
  starting transfers between devices: 5.35 us -> 0 us
    pallas_call x0 -> x2, Pallas kernels: none -> 81.2 us  [the longest x1 50 us: exchange(): pl.pallas_call(exchange_kernel, out_shape=(jax.ShapeDtypeStruct((4, tok_d...]
    all_gather x1 -> x0, waiting for transfers between devices: 61.8 us -> none  [on_device(): bank = lax.all_gather(own_bank, 'ep', axis=0, tiled=True)]
    reduce_scatter x1 -> x0, waiting for transfers between devices: 34.7 us -> none  [on_device(): lax.psum_scatter(jnp.dot(attended, w_out, preferred_element_type=jnp.floa...]
    all_to_all x1 -> x0, waiting for transfers between devices: 17.9 us -> none  [on_device(): lax.all_to_all(qkv, 'tok', split_axis=1, concat_axis=0, tiled=True)]
    pallas_call x1, Pallas kernels: 238 us -> 231 us  [routed_experts(): pl.pallas_call(functools.partial(routed_kernel, dims), out_shape=jax.Shap...]
    all_to_all x1 -> x0, starting transfers between devices: 5.31 us -> none  [on_device(): lax.all_to_all(qkv, 'tok', split_axis=1, concat_axis=0, tiled=True)]
  transfers between devices with their start and end apart: 3 -> 0, of which waited for: 3 -> 0; matrix products, arithmetic and copies ran while one was open for 0% -> 0% of each run, Pallas kernels for 0% -> 0%
where the time goes in v3:
time: 354 us; the launch traced here: 347 us
  Pallas kernels  336 us (95%)
  local copies, waits for them, and re-layouts  8.42 us (2%)
    pallas_call x1, Pallas kernels, routed_experts(): pl.pallas_call(functools.partial(routed_kernel, dims), out_shape=jax.Shap...  231 us
    pallas_call x1, Pallas kernels, exchange(): pl.pallas_call(exchange_kernel, out_shape=(jax.ShapeDtypeStruct((4, tok_d...  50 us
    pallas_call x1, Pallas kernels, project(): pl.pallas_call(project_kernel, out_shape=(jax.ShapeDtypeStruct(resid.shap...  31.2 us
    pallas_call x1, Pallas kernels, attention(): pl.pallas_call(functools.partial(attention_kernel, tok_dev, segs, most_st...  24 us

profile of v3, /device:TPU:8, one launch (start us, length us, event | category | flops | bytes accessed | tf_op | source)
XLA Modules:
  0.0 347.0 jit_solution(3296602340401581455)
XLA Ops:
  0.0 0.7 convert.5
  0.7 0.6 broadcast_in_dim.24.slots_ref
  1.3 0.7 copy.17
  2.1 0.1 reduce
  2.2 0.7 sub.6
  2.8 0.7 pad_add_fusion.seg_ref
  3.6 0.1 broadcast_add_fusion
  3.6 0.1 add.45
  3.7 0.0 copy-start.3
  3.8 50.0 %exchange.1 = (bf16[4,128,1024]{2,1,0:T(8,128)(2,1)}, bf16[2560,256]{1,0:T(8,128)(2,1)}, bf16[8704,256]{1,0:T(8,128)(2,1)}) custom-call(bf16[128,5120]{1,0:T(8,128)(2,1)} %qkv_ref.1, bf16[256,256]{1,0:T(8,128)(2,1)} %bitcast.10, bf16[16,256]{1,0:T(8,128)(2,1)} %broadcast_in_dim.24.slots_ref), custom_call_target="tpu_custom_call" | custom-call | bytes 83886080 | tf_op jit(solution)/shard_map/exchange/pallas_call | solution.py:334
  53.8 0.0 copy-start.4
  53.8 0.9 slice.4
  54.7 0.1 reshape.68
  54.8 0.1 select_reduce_fusion.row_ref
  54.9 0.0 copy-start
  54.9 1.3 copy-done
  56.2 0.0 copy-start.1
  56.2 1.2 copy-done.1
  57.4 0.0 copy-start.2
  57.4 24.0 %attend.1.attended_ref = bf16[4,128,1024]{2,1,0:T(8,128)(2,1)S(1)} custom-call(s32[52]{0:T(128)S(1)} %pad_add_fusion.seg_ref, s32[128]{0:T(128)S(1)} %select_reduce_fusion.row_ref, bf16[4,128,1024]{2,1,0:T(8,128)(2,1)S(1)} %copy-done.1, bf16[2560,256]{1,0:T(8,128)(2,1)S(1)} %copy-done, bf16[8704,256]{1,0:T(8,128)(2,1)} %get-tuple-element.10.bank_ref), custom_call_target="tpu_custom_call" | custom-call | tf_op jit(solution)/shard_map/attend/pallas_call | solution.py:130
  81.4 0.0 copy-done.3
  81.4 0.0 copy-done.4
  81.4 0.0 copy-done.2
  81.4 31.2 %project.1 = (bf16[128,2048]{1,0:T(8,128)(2,1)S(1)}, bf16[128,2048]{1,0:T(8,128)(2,1)S(1)}) custom-call(bf16[4,128,1024]{2,1,0:T(8,128)(2,1)S(1)} %attend.1.attended_ref, bf16[1024,2048]{1,0:T(8,128)(2,1)S(1)} %copy-done.2, bf16[128,2048]{1,0:T(8,128)(2,1)S(1)} %copy-done.3, f32[1,2048]{1,0:T(1,128)S(1)} %bitcast.8), custom_call_target="tpu_custom_call" | custom-call | flops 2147483648 | bytes 41943040 | tf_op jit(solution)/shard_map/project/pallas_call | solution.py:423
  112.6 0.0 copy-start.5
  112.6 0.8 copy-done.5
  113.4 0.0 copy-start.6
  113.4 0.8 copy-done.6
  114.2 230.8 %routed_experts.1 = bf16[128,2048]{1,0:T(8,128)(2,1)} custom-call(bf16[128,2048]{1,0:T(8,128)(2,1)} %copy-done.6, bf16[128,2048]{1,0:T(8,128)(2,1)} %copy-done.5, s32[8,128]{1,0:T(8,128)} %bitcast.12, f32[8,128]{1,0:T(8,128)} %bitcast.13, bf16[1,2048,1536]{2,1,0:T(8,128)(2,1)} %gate_up_hbm.1, bf16[1,768,2048]{2,1,0:T(8,128)(2,1)} %down_hbm.1), custom_call_target="tpu_custom_call" | custom-call | flops 21474836480 | bytes 50331648 | tf_op jit(solution)/shard_map/routed_experts/pallas_call | solution.py:613
  345.1 1.9 copy.22
  (6 shorter events, 0.1 us)
Async XLA Ops:
  3.7 77.7 %copy-start.3 = (bf16[128,2048]{1,0:T(8,128)(2,1)S(1)}, bf16[128,2048]{1,0:T(8,128)(2,1)}, u32[]{:S(2)}) copy-start(bf16[128,2048]{1,0:T(8,128)(2,1)} %resid_ref.1) | copy-start | bytes 1572868
  53.8 27.7 %copy-start.4 = (f32[2048]{0:T(1024)S(1)}, f32[2048]{0:T(1024)}, u32[]{:S(2)}) copy-start(f32[2048]{0:T(1024)} %param.19) | copy-start | bytes 24580
  54.9 1.3 copy-start
  56.2 1.2 copy-start.1
  57.4 24.0 %copy-start.2 = (bf16[1024,2048]{1,0:T(8,128)(2,1)S(1)}, bf16[1024,2048]{1,0:T(8,128)(2,1)}, u32[]{:S(2)}) copy-start(bf16[1024,2048]{1,0:T(8,128)(2,1)} %weight_ref.1) | copy-start | bytes 12582916
  112.6 0.8 copy-start.5
  113.4 0.8 copy-start.6

commit v4 on v3

--- a/solution.py
+++ b/solution.py
@@ -438,203 +438,319 @@
 
 
 CAP = 16
-GROUP = 16
-MIX = 37
-
-def hop(dims, step, way):
-    deep, tall, wide, cores = dims
-    total = deep * tall * wide * cores
-    offset = lax.rem(step * MIX, total)
+SIDE = 4
+PLANE = 32
+CUTS = ((0, 768), (768, 640), (1408, 640))
+
+
+def position():
     tok, ep = lax.axis_index("tok"), lax.axis_index("ep")
-    sizes = (deep, tall, wide, cores)
-    mine = (tok, lax.div(ep, wide * cores), lax.rem(lax.div(ep, cores), wide), lax.rem(ep, cores))
-    strides = (tall * wide * cores, wide * cores, cores, 1)
-    at = [
-        lax.rem(own + size + way * lax.rem(lax.div(offset, stride), size), size)
-        for own, size, stride in zip(mine, sizes, strides)
-    ]
-    place = (at[1] * wide + at[2]) * cores + at[3]
-    return (at[0], place), at[0] * (tall * wide * cores) + place
+    return tok, lax.div(ep, 8), lax.rem(lax.div(ep, 2), 4), lax.rem(ep, 2)
+
+
+def moved(offsets, way):
+    at = [lax.rem(own + size + way * off, size) for own, off, size in zip(position(), offsets, (4, 4, 4, 2))]
+    return at[0], (at[1] * 4 + at[2]) * 2 + at[3]
+
+
+def plane_offsets(cut, index, div, rem):
+    core, outer, inner = div(index, 16), rem(div(index, 4), 4), rem(index, 4)
+    return ((0, inner, outer, core), (inner, 0, outer, core), (outer, inner, 0, core))[cut]
+
+
+def line_offsets(cut, turn):
+    return tuple(turn if axis == cut else 0 for axis in range(3)) + (0,)
 
 
 def routed_kernel(
-    dims, normed_ref, mixed_ref, routes_ref, probs_ref, gate_up_hbm, down_hbm, out_ref,
-    stage, arrived, back, gate_up, down, rank, share, pick, total,
-    weight_sems, send_sems, recv_sems, back_send_sems, back_recv_sems,
+    normed_ref, mixed_ref, table_ref, gate_up_hbm, down_hbm, out_ref,
+    line0, line1, line2, stage0, stage1, stage2, came0, came1, came2, back0, back1, back2,
+    part0, part1, part2, inbox0, inbox1, inbox2, sum0, sum1, sum2,
+    gate_up, down, tables, rank, share, pick, rows_in,
+    weight_sems, table_sems, line_send, line_recv, out_send, near_recv, far_recv, home_send, home_recv,
+    part_send, part_recv,
 ):
-    devices = dims[0] * dims[1] * dims[2] * dims[3]
-    chunks = devices // GROUP
-    rows = GROUP * CAP
+    lines, stages, cames, backs = (line0, line1, line2), (stage0, stage1, stage2), (came0, came1, came2), (back0, back1, back2)
+    parts, inboxes, sums = (part0, part1, part2), (inbox0, inbox1, inbox2), (sum0, sum1, sum2)
     tokens = normed_ref.shape[0]
-    hidden_width = down.shape[0]
+    width = down.shape[0]
+    devices = SIDE * PLANE
+    message = SIDE * CAP
     load_gate_up = pltpu.make_async_copy(gate_up_hbm.at[0], gate_up, weight_sems.at[0])
     load_down = pltpu.make_async_copy(down_hbm.at[0], down, weight_sems.at[1])
     load_gate_up.start()
     load_down.start()
-
     barrier = pltpu.get_barrier_semaphore()
 
     def greet(step, ignored):
-        pl.semaphore_signal(barrier, inc=1, device_id=hop(dims, step, 1)[0], device_id_type=MESH)
+        offsets = (lax.div(step, 32), lax.rem(lax.div(step, 8), 4), lax.rem(lax.div(step, 2), 4), lax.rem(step, 2))
+        pl.semaphore_signal(barrier, inc=1, device_id=moved(offsets, 1), device_id_type=MESH)
         return ignored
 
     lax.fori_loop(1, devices, greet, 0)
-
-    experts = lax.broadcasted_iota(jnp.int32, (devices, tokens), 0)
-    probs = probs_ref[...]
-    shares = probs / jnp.sum(probs, axis=0, keepdims=True)
-    named = jnp.zeros((devices, tokens), jnp.float32)
-    owed = jnp.zeros((devices, tokens), jnp.float32)
-    for k in range(routes_ref.shape[0]):
-        match = experts == routes_ref[k : k + 1, :]
-        named = jnp.where(match, 1.0, named)
-        owed = jnp.where(match, shares[k : k + 1, :], owed)
+    for cut, (start, size) in enumerate(CUTS):
+        lines[cut][:tokens] = normed_ref[:, start : start + size]
+        tables[cut, 0] = table_ref[...]
+    pl.semaphore_wait(barrier, devices - 1)
+
+    def remote(source, place, send_sem, recv_sem, device):
+        return pltpu.make_async_remote_copy(
+            src_ref=source, dst_ref=place, send_sem=send_sem, recv_sem=recv_sem, device_id=device, device_id_type=MESH
+        )
+
+    def rows_of(ref, start, size):
+        return ref.at[pl.ds(pl.multiple_of(start, CAP), size)]
+
+    def settle(ref, size, sem):
+        pltpu.make_async_copy(ref.at[pl.ds(0, size)], ref.at[pl.ds(0, size)], sem).wait()
+
+    for cut in range(3):
+        for turn in range(1, SIDE):
+            remote(
+                table_ref, tables.at[cut, turn], table_sems.at[0], table_sems.at[1], moved(line_offsets(cut, turn), 1)
+            ).start()
+    for cut in range(3):
+        for turn in range(1, SIDE):
+            remote(
+                rows_of(lines[cut], 0, tokens), rows_of(lines[cut], turn * tokens, tokens),
+                line_send.at[cut], line_recv.at[cut], moved(line_offsets(cut, turn), 1),
+            ).start()
+
+    pltpu.make_async_copy(tables.at[:, pl.ds(0, 3)], tables.at[:, pl.ds(0, 3)], table_sems.at[1]).wait()
     before = (
         lax.broadcasted_iota(jnp.int32, (tokens, tokens), 0) < lax.broadcasted_iota(jnp.int32, (tokens, tokens), 1)
     ).astype(jnp.bfloat16)
-    earlier = jnp.dot(named.astype(jnp.bfloat16), before, preferred_element_type=jnp.float32)
-    rank[...] = jnp.where(named > 0.0, earlier, -1.0)
-    share[...] = owed
+    index = lax.broadcasted_iota(jnp.int32, (PLANE, tokens), 0)
+    shift = {16: 4, 4: 2}
+    top = table_ref.shape[0] // 2
+    for cut in range(3):
+        offsets = plane_offsets(cut, index, lambda v, d: v >> shift[d], lambda v, d: v & (d - 1))
+        z, y, x, c = [(own + off) & (size - 1) for own, off, size in zip(position(), offsets, (4, 4, 4, 2))]
+        expert = (z * 32 + y * 8 + x * 2 + c).astype(jnp.float32)
+        for turn in range(SIDE):
+            probs = tables[cut, turn, top:, :]
+            shares = probs / jnp.sum(probs, axis=0, keepdims=True)
+            named = jnp.zeros((PLANE, tokens), jnp.float32)
+            owed = jnp.zeros((PLANE, tokens), jnp.float32)
+            for k in range(top):
+                match = expert == tables[cut, turn, k : k + 1, :]
+                named = jnp.where(match, 1.0, named)
+                owed = jnp.where(match, shares[k : k + 1, :], owed)
+            earlier = jnp.dot(named.astype(jnp.bfloat16), before, preferred_element_type=jnp.float32)
+            at = (cut * SIDE + turn) * PLANE
+            rank[at : at + PLANE, :] = jnp.where(named > 0.0, earlier, -1.0)
+            share[at : at + PLANE, :] = owed
+
     slot = lax.broadcasted_iota(jnp.int32, (CAP, tokens), 0).astype(jnp.float32)
 
-    def slab(ref, step):
-        return ref.at[pl.ds(pl.multiple_of(step * CAP, CAP), CAP)]
-
-    def block(ref, chunk):
-        return ref.at[pl.ds(pl.multiple_of(chunk * rows, rows), rows)]
-
-    pl.semaphore_wait(barrier, devices - 1)
-
-    def dispatch(chunk, ignored):
-        def choose(j, inner):
-            expert = hop(dims, chunk * GROUP + j, 1)[1]
-            pick[pl.ds(pl.multiple_of(j * CAP, CAP), CAP), :] = jnp.where(
-                rank[pl.ds(expert, 1), :] == slot, 1.0, 0.0
+    def choose(cut, core, turn, weighted):
+        for j in range(16):
+            at = (cut * SIDE + turn) * PLANE + core * 16 + j
+            chosen = share[pl.ds(at, 1), :] if weighted else 1.0
+            pick[j * CAP : (j + 1) * CAP, :] = jnp.where(rank[pl.ds(at, 1), :] == slot, chosen, 0.0).astype(jnp.bfloat16)
+
+    def send(cut, i, recv_sem):
+        source, place = rows_of(stages[cut], i * message, message), rows_of(cames[cut], i * message, message)
+        offsets = plane_offsets(cut, i, lax.div, lax.rem)
+
+        @pl.when(i == 0)
+        def _():
+            pltpu.make_async_copy(source, place, recv_sem).start()
+
+        @pl.when(i > 0)
+        def _():
+            remote(source, place, out_send.at[cut], recv_sem, moved(offsets, 1)).start()
+
+    def fill(cut, core):
+        def one_shard(turn, ignored):
+            choose(cut, core, turn, False)
+            found = jnp.dot(
+                pick[...], rows_of(lines[cut], turn * tokens, tokens)[...], preferred_element_type=jnp.float32
             ).astype(jnp.bfloat16)
+            for j in range(16):
+                rows_of(stages[cut], (core * 16 + j) * message + turn * CAP, CAP)[...] = found[j * CAP : (j + 1) * CAP]
+            return ignored
+
+        lax.fori_loop(0, SIDE, one_shard, 0)
+
+    def dispatch(core, ignored):
+        fill(2, core)
+
+        def send_far(j, inner):
+            send(2, core * 16 + j, far_recv.at[core])
             return inner
 
-        lax.fori_loop(0, GROUP, choose, 0)
-        block(stage, chunk)[...] = jnp.dot(
-            pick[...], normed_ref[...], preferred_element_type=jnp.float32
-        ).astype(jnp.bfloat16)
-
-        def send(j, inner):
-            step = chunk * GROUP + j
-
-            @pl.when(step > 0)
-            def _():
-                pltpu.make_async_remote_copy(
-                    src_ref=slab(stage, step), dst_ref=slab(arrived, step),
-                    send_sem=send_sems.at[chunk], recv_sem=recv_sems.at[chunk],
-                    device_id=hop(dims, step, 1)[0], device_id_type=MESH,
-                ).start()
-
-            @pl.when(step == 0)
-            def _():
-                pltpu.make_async_copy(slab(stage, step), slab(arrived, step), recv_sems.at[chunk]).start()
-
+        lax.fori_loop(0, 16, send_far, 0)
+        fill(0, core)
+        fill(1, core)
+
+        def send_near(j, inner):
+            chunk = core * 4 + lax.div(j, 4)
+            send(0, core * 16 + j, near_recv.at[0, chunk])
+            send(1, core * 16 + j, near_recv.at[1, chunk])
             return inner
 
-        return lax.fori_loop(0, GROUP, send, ignored)
-
-    lax.fori_loop(0, chunks, dispatch, 0)
+        return lax.fori_loop(0, 16, send_near, ignored)
+
+    for cut in range(3):
+        settle(lines[cut], 3 * tokens, line_recv.at[cut])
+    lax.fori_loop(0, 2, dispatch, 0)
     load_gate_up.wait()
     load_down.wait()
+    block = SIDE * message
+
+    def slab1(chunk, j):
+        return rows_of(came1, chunk * block + (j % 4) * message + (j // 4) * CAP, CAP)
+
+    def slab2(chunk, j):
+        core, wide = lax.div(chunk, 4), lax.rem(chunk, 4)
+        return rows_of(came2, (core * 16 + (j % 4) * 4 + j // 4) * message + wide * CAP, CAP)
+
+    def give(cut, i):
+        source, place = rows_of(cames[cut], i * message, message), rows_of(backs[cut], i * message, message)
+        offsets = plane_offsets(cut, i, lax.div, lax.rem)
+        recv_sem = home_recv.at[cut, lax.div(i, 16)]
+
+        @pl.when(i == 0)
+        def _():
+            pltpu.make_async_copy(source, place, recv_sem).start()
+
+        @pl.when(i > 0)
+        def _():
+            remote(source, place, home_send.at[cut], recv_sem, moved(offsets, -1)).start()
 
     def work(chunk, ignored):
-        pltpu.make_async_copy(block(arrived, chunk), block(arrived, chunk), recv_sems.at[chunk]).wait()
-        came = block(arrived, chunk)[...]
-        gate = jnp.dot(came, gate_up[:, :hidden_width], preferred_element_type=jnp.float32)
-        up = jnp.dot(came, gate_up[:, hidden_width:], preferred_element_type=jnp.float32)
+        @pl.when(lax.rem(chunk, 4) == 0)
+        def _():
+            settle(came2, 16 * message, far_recv.at[lax.div(chunk, 4)])
+
+        settle(came0, block, near_recv.at[0, chunk])
+        settle(came1, block, near_recv.at[1, chunk])
+        rows_in[:, 0:768] = rows_of(came0, chunk * block, block)[...]
+        for j in range(16):
+            rows_in[j * CAP : (j + 1) * CAP, 768:1408] = slab1(chunk, j)[...]
+            rows_in[j * CAP : (j + 1) * CAP, 1408:2048] = slab2(chunk, j)[...]
+        gate = jnp.dot(rows_in[...], gate_up[:, :width], preferred_element_type=jnp.float32)
+        up = jnp.dot(rows_in[...], gate_up[:, width:], preferred_element_type=jnp.float32)
         hidden = (gate * jax.nn.sigmoid(gate) * up).astype(jnp.bfloat16)
-        block(arrived, chunk)[...] = jnp.dot(hidden, down[...], preferred_element_type=jnp.float32).astype(jnp.bfloat16)
-
-        def give_back(j, inner):
-            step = chunk * GROUP + j
-
-            @pl.when(step > 0)
+        made = jnp.dot(hidden, down[...], preferred_element_type=jnp.float32).astype(jnp.bfloat16)
+        rows_of(came0, chunk * block, block)[...] = made[:, 0:768]
+        for j in range(16):
+            slab1(chunk, j)[...] = made[j * CAP : (j + 1) * CAP, 768:1408]
+            slab2(chunk, j)[...] = made[j * CAP : (j + 1) * CAP, 1408:2048]
+
+        def give_near(j, inner):
+            give(0, chunk * 4 + j)
+            give(1, chunk * 4 + j)
+            return inner
+
+        lax.fori_loop(0, 4, give_near, 0)
+
+        @pl.when(lax.rem(chunk, 4) == 3)
+        def _():
+            def give_far(j, inner):
+                give(2, lax.div(chunk, 4) * 16 + j)
+                return inner
+
+            lax.fori_loop(0, 16, give_far, 0)
+
+        return ignored
+
+    lax.fori_loop(0, 8, work, 0)
+
+    for cut in range(3):
+        sums[cut][...] = jnp.zeros_like(sums[cut])
+
+    def combine(core, ignored):
+        for cut in range(3):
+            settle(backs[cut], 16 * message, home_recv.at[cut, core])
+
+            def one_shard(turn, inner):
+                choose(cut, core, turn, True)
+                found = jnp.concatenate(
+                    [rows_of(backs[cut], (core * 16 + j) * message + turn * CAP, CAP)[...] for j in range(16)], axis=0
+                )
+                total = rows_of(sums[cut], turn * tokens, tokens)
+                total[...] += lax.dot_general(
+                    pick[...], found, (((0,), (0,)), ((), ())), preferred_element_type=jnp.float32
+                )
+                return inner
+
+            lax.fori_loop(0, SIDE, one_shard, 0)
+
+            @pl.when(core == 1)
             def _():
-                pltpu.make_async_remote_copy(
-                    src_ref=slab(arrived, step), dst_ref=slab(back, step),
-                    send_sem=back_send_sems.at[chunk], recv_sem=back_recv_sems.at[chunk],
-                    device_id=hop(dims, step, -1)[0], device_id_type=MESH,
-                ).start()
-
-            @pl.when(step == 0)
-            def _():
-                pltpu.make_async_copy(slab(arrived, step), slab(back, step), back_recv_sems.at[chunk]).start()
-
-            return inner
-
-        return lax.fori_loop(0, GROUP, give_back, ignored)
-
-    lax.fori_loop(0, chunks, work, 0)
-    total[...] = mixed_ref[...].astype(jnp.float32)
-
-    def combine(chunk, ignored):
-        def owe(j, inner):
-            expert = hop(dims, chunk * GROUP + j, 1)[1]
-            pick[pl.ds(pl.multiple_of(j * CAP, CAP), CAP), :] = jnp.where(
-                rank[pl.ds(expert, 1), :] == slot, share[pl.ds(expert, 1), :], 0.0
-            ).astype(jnp.bfloat16)
-            return inner
-
-        lax.fori_loop(0, GROUP, owe, 0)
-        pltpu.make_async_copy(block(back, chunk), block(back, chunk), back_recv_sems.at[chunk]).wait()
-        total[...] += lax.dot_general(
-            pick[...], block(back, chunk)[...], (((0,), (0,)), ((), ())), preferred_element_type=jnp.float32
-        )
+                parts[cut][...] = sums[cut][...].astype(jnp.bfloat16)
+                for turn in range(1, SIDE):
+                    remote(
+                        rows_of(parts[cut], turn * tokens, tokens), rows_of(inboxes[cut], turn * tokens, tokens),
+                        part_send.at[cut], part_recv.at[cut], moved(line_offsets(cut, turn), -1),
+                    ).start()
+
         return ignored
 
-    lax.fori_loop(0, chunks, combine, 0)
-    out_ref[...] = total[...].astype(jnp.bfloat16)
-
-    own = CAP
-    first = pl.ds(own, rows - own)
-    pltpu.make_async_copy(stage.at[first], stage.at[first], send_sems.at[0]).wait()
-    pltpu.make_async_copy(stage.at[first], stage.at[first], back_send_sems.at[0]).wait()
-
-    def settle(chunk, ignored):
-        pltpu.make_async_copy(block(stage, chunk), block(stage, chunk), send_sems.at[chunk]).wait()
-        pltpu.make_async_copy(block(stage, chunk), block(stage, chunk), back_send_sems.at[chunk]).wait()
-        return ignored
-
-    lax.fori_loop(1, chunks, settle, 0)
-
-
-def routed_experts(dims, normed, mixed, routes, probs, gate_up, down):
-    devices = dims[0] * dims[1] * dims[2] * dims[3]
-    chunks = devices // GROUP
+    lax.fori_loop(0, 2, combine, 0)
+    for cut, (start, size) in enumerate(CUTS):
+        settle(inboxes[cut], 3 * tokens, part_recv.at[cut])
+        total = mixed_ref[:, start : start + size].astype(jnp.float32) + sums[cut][:tokens]
+        for turn in range(1, SIDE):
+            total = total + inboxes[cut][turn * tokens : (turn + 1) * tokens].astype(jnp.float32)
+        out_ref[:, start : start + size] = total.astype(jnp.bfloat16)
+    pltpu.make_async_copy(tables.at[:, pl.ds(0, 3)], tables.at[:, pl.ds(0, 3)], table_sems.at[0]).wait()
+    for cut in range(3):
+        settle(lines[cut], 3 * tokens, line_send.at[cut])
+        settle(stages[cut], (PLANE - 1) * message, out_send.at[cut])
+        settle(stages[cut], (PLANE - 1) * message, home_send.at[cut])
+        settle(lines[cut], 3 * tokens, part_send.at[cut])
+
+
+def routed_experts(normed, mixed, routes, probs, gate_up, down):
     tokens, width = normed.shape
-    slots = devices * CAP
     vmem = pl.BlockSpec(memory_space=pltpu.VMEM)
     kept = pl.BlockSpec(memory_space=pl.ANY)
+    slots = SIDE * PLANE * CAP
     flops = 2 * slots * width * (down.shape[1] * 3 + 2 * tokens)
+    table = jnp.concatenate([routes.T.astype(jnp.float32), probs.T], axis=0)
+
+    def each(rows, kind):
+        return [pltpu.VMEM((rows, size), kind) for start, size in CUTS]
+
     return pl.pallas_call(
-        functools.partial(routed_kernel, dims),
+        routed_kernel,
         out_shape=jax.ShapeDtypeStruct(mixed.shape, jnp.bfloat16),
-        in_specs=[vmem] * 4 + [kept] * 2,
+        in_specs=[vmem] * 3 + [kept] * 2,
         out_specs=vmem,
-        scratch_shapes=[
-            pltpu.VMEM((slots, width), jnp.bfloat16),
-            pltpu.VMEM((slots, width), jnp.bfloat16),
-            pltpu.VMEM((slots, width), jnp.bfloat16),
+        scratch_shapes=each(SIDE * tokens, jnp.bfloat16)
+        + each(slots, jnp.bfloat16)
+        + each(slots, jnp.bfloat16)
+        + each(slots, jnp.bfloat16)
+        + each(SIDE * tokens, jnp.bfloat16)
+        + each(SIDE * tokens, jnp.bfloat16)
+        + each(SIDE * tokens, jnp.float32)
+        + [
             pltpu.VMEM(gate_up.shape[1:], jnp.bfloat16),
             pltpu.VMEM(down.shape[1:], jnp.bfloat16),
-            pltpu.VMEM((devices, tokens), jnp.float32),
-            pltpu.VMEM((devices, tokens), jnp.float32),
-            pltpu.VMEM((GROUP * CAP, tokens), jnp.bfloat16),
-            pltpu.VMEM((tokens, width), jnp.float32),
+            pltpu.VMEM((3, SIDE, 2 * routes.shape[1], tokens), jnp.float32),
+            pltpu.VMEM((3 * SIDE * PLANE, tokens), jnp.float32),
+            pltpu.VMEM((3 * SIDE * PLANE, tokens), jnp.float32),
+            pltpu.VMEM((16 * CAP, tokens), jnp.bfloat16),
+            pltpu.VMEM((16 * CAP, width), jnp.bfloat16),
             pltpu.SemaphoreType.DMA((2,)),
-            pltpu.SemaphoreType.DMA((chunks,)),
-            pltpu.SemaphoreType.DMA((chunks,)),
-            pltpu.SemaphoreType.DMA((chunks,)),
-            pltpu.SemaphoreType.DMA((chunks,)),
+            pltpu.SemaphoreType.DMA((2,)),
+            pltpu.SemaphoreType.DMA((3,)),
+            pltpu.SemaphoreType.DMA((3,)),
+            pltpu.SemaphoreType.DMA((3,)),
+            pltpu.SemaphoreType.DMA((2, 8)),
+            pltpu.SemaphoreType.DMA((2,)),
+            pltpu.SemaphoreType.DMA((3,)),
+            pltpu.SemaphoreType.DMA((3, 2)),
+            pltpu.SemaphoreType.DMA((3,)),
+            pltpu.SemaphoreType.DMA((3,)),
         ],
-        compiler_params=pltpu.CompilerParams(collective_id=0, has_side_effects=True, vmem_limit_bytes=56 << 20),
+        compiler_params=pltpu.CompilerParams(collective_id=0, has_side_effects=True, vmem_limit_bytes=58 << 20),
         cost_estimate=pl.CostEstimate(flops=flops, bytes_accessed=6 * slots * width * 2, transcendentals=0),
         name="routed_experts",
-    )(normed, mixed, routes.T, probs.T, gate_up, down)
+    )(normed, mixed, table, gate_up, down)
 
 
 def on_device(
@@ -651,7 +767,6 @@
     w_gate_up,
     w_down,
 ):
-    tok_groups = lax.axis_size("tok")
     ep_count = lax.axis_size("ep")
     tok_dev = resid.shape[0]
     seg_count = seg_lengths.shape[0]
@@ -674,8 +789,7 @@
     seg_table = jnp.concatenate([seg_ends - seg_lengths, seg_ends, cache_age, first_tokens]).astype(jnp.int32)
     attended = attention(seg_table, row_table, queries, window, bank, seg_count, SEG_MOST)
     mixed, normed = project(attended, w_out, resid, norm_gain)
-    dims = (tok_groups, ep_count // 8, 4, 2)
-    return routed_experts(dims, normed, mixed, routes, route_probs, w_gate_up, w_down)
+    return routed_experts(normed, mixed, routes, route_probs, w_gate_up, w_down)
 
 
 def solution(mesh):

time: 354 us -> 311 us (0.88)
  Pallas kernels: 336 us -> 295 us
    pallas_call x1, Pallas kernels: 231 us -> 195 us  [routed_experts(): pl.pallas_call(routed_kernel, out_shape=jax.ShapeDtypeStruct(mixed.shape,...]
    pallas_call x1, Pallas kernels: 24 us -> 19.2 us  [attention(): pl.pallas_call(functools.partial(attention_kernel, tok_dev, segs, most_st...]
where the time goes in v4:
time: 311 us; the launch traced here: 307 us
  Pallas kernels  295 us (95%)
  local copies, waits for them, and re-layouts  8.44 us (3%)
    pallas_call x1, Pallas kernels, routed_experts(): pl.pallas_call(routed_kernel, out_shape=jax.ShapeDtypeStruct(mixed.shape,...  195 us
    pallas_call x1, Pallas kernels, exchange(): pl.pallas_call(exchange_kernel, out_shape=(jax.ShapeDtypeStruct((4, tok_d...  49.9 us
    pallas_call x1, Pallas kernels, project(): pl.pallas_call(project_kernel, out_shape=(jax.ShapeDtypeStruct(resid.shap...  31.3 us
    pallas_call x1, Pallas kernels, attention(): pl.pallas_call(functools.partial(attention_kernel, tok_dev, segs, most_st...  19.2 us

profile of v4, /device:TPU:8, one launch (start us, length us, event | category | flops | bytes accessed | tf_op | source)
XLA Modules:
  0.0 307.0 jit_solution(16252962960219734775)
XLA Ops:
  0.0 0.7 copy.17
  0.8 0.1 reduce
  0.9 0.7 sub.6
  1.6 0.7 pad_add_fusion.seg_ref
  2.3 0.7 convert.5
  3.0 0.6 broadcast_in_dim.24.slots_ref
  3.6 0.0 copy-start.3
  3.6 49.9 %exchange.1 = (bf16[4,128,1024]{2,1,0:T(8,128)(2,1)}, bf16[2560,256]{1,0:T(8,128)(2,1)}, bf16[8704,256]{1,0:T(8,128)(2,1)}) custom-call(bf16[128,5120]{1,0:T(8,128)(2,1)} %qkv_ref.1, bf16[256,256]{1,0:T(8,128)(2,1)} %bitcast.11, bf16[16,256]{1,0:T(8,128)(2,1)} %broadcast_in_dim.24.slots_ref), custom_call_target="tpu_custom_call" | custom-call | bytes 83886080 | tf_op jit(solution)/shard_map/exchange/pallas_call | solution.py:334
  53.5 0.0 copy-start.4
  53.5 0.9 slice.4
  54.4 0.1 reshape.68
  54.5 0.1 broadcast_add_fusion
  54.6 0.1 add.45
  54.7 0.1 select_reduce_fusion.row_ref
  54.8 0.0 copy-start
  54.8 1.3 copy-done
  56.1 0.0 copy-start.1
  56.1 1.2 copy-done.1
  57.4 0.0 copy-start.2
  57.4 19.2 %attend.1.attended_ref = bf16[4,128,1024]{2,1,0:T(8,128)(2,1)S(1)} custom-call(s32[52]{0:T(128)S(1)} %pad_add_fusion.seg_ref, s32[128]{0:T(128)S(1)} %select_reduce_fusion.row_ref, bf16[4,128,1024]{2,1,0:T(8,128)(2,1)S(1)} %copy-done.1, bf16[2560,256]{1,0:T(8,128)(2,1)S(1)} %copy-done, bf16[8704,256]{1,0:T(8,128)(2,1)} %get-tuple-element.10.bank_ref), custom_call_target="tpu_custom_call" | custom-call | tf_op jit(solution)/shard_map/attend/pallas_call | solution.py:130
  76.5 0.0 copy-start.7
  76.5 0.0 copy-start.8
  76.6 0.0 copy-done.3
  76.6 0.0 copy-done.4
  76.6 0.0 copy-done.2
  76.6 31.3 %project.1 = (bf16[128,2048]{1,0:T(8,128)(2,1)S(1)}, bf16[128,2048]{1,0:T(8,128)(2,1)S(1)}) custom-call(bf16[4,128,1024]{2,1,0:T(8,128)(2,1)S(1)} %attend.1.attended_ref, bf16[1024,2048]{1,0:T(8,128)(2,1)S(1)} %copy-done.2, bf16[128,2048]{1,0:T(8,128)(2,1)S(1)} %copy-done.3, f32[1,2048]{1,0:T(1,128)S(1)} %bitcast.9), custom_call_target="tpu_custom_call" | custom-call | flops 2147483648 | bytes 41943040 | tf_op jit(solution)/shard_map/project/pallas_call | solution.py:423
  107.9 0.0 copy-start.5
  108.0 0.8 copy-done.5
  108.7 0.0 copy-start.6
  108.7 0.8 copy-done.6
  109.5 0.0 copy-done.7
  109.5 0.0 copy-done.8
  109.5 0.6 pad_maximum_fusion.table_ref
  110.1 194.9 %routed_experts.1 = bf16[128,2048]{1,0:T(8,128)(2,1)} custom-call(bf16[128,2048]{1,0:T(8,128)(2,1)} %copy-done.6, bf16[128,2048]{1,0:T(8,128)(2,1)} %copy-done.5, f32[16,128]{1,0:T(8,128)} %pad_maximum_fusion.table_ref, bf16[1,2048,1536]{2,1,0:T(8,128)(2,1)} %gate_up_hbm.1, bf16[1,768,2048]{2,1,0:T(8,128)(2,1)} %down_hbm.1), custom_call_target="tpu_custom_call" | custom-call | flops 21474836480 | bytes 50331648 | tf_op jit(solution)/shard_map/routed_experts/pallas_call | solution.py:718
  305.1 1.9 copy.22
  (7 shorter events, 0.1 us)
Async XLA Ops:
  3.6 73.0 %copy-start.3 = (bf16[128,2048]{1,0:T(8,128)(2,1)S(1)}, bf16[128,2048]{1,0:T(8,128)(2,1)}, u32[]{:S(2)}) copy-start(bf16[128,2048]{1,0:T(8,128)(2,1)} %resid_ref.1) | copy-start | bytes 1572868
  53.5 23.1 %copy-start.4 = (f32[2048]{0:T(1024)S(1)}, f32[2048]{0:T(1024)}, u32[]{:S(2)}) copy-start(f32[2048]{0:T(1024)} %param.19) | copy-start | bytes 24580
  54.8 1.3 copy-start
  56.1 1.2 copy-start.1
  57.4 19.2 %copy-start.2 = (bf16[1024,2048]{1,0:T(8,128)(2,1)S(1)}, bf16[1024,2048]{1,0:T(8,128)(2,1)}, u32[]{:S(2)}) copy-start(bf16[1024,2048]{1,0:T(8,128)(2,1)} %weight_ref.1) | copy-start | bytes 12582916
  76.5 33.0 %copy-start.7 = (s32[128,8]{0,1:T(8,128)S(1)}, s32[128,8]{0,1:T(8,128)}, u32[]{:S(2)}) copy-start(s32[128,8]{0,1:T(8,128)} %param.20) | copy-start | bytes 12292
  76.5 33.0 %copy-start.8 = (f32[128,8]{0,1:T(8,128)S(1)}, f32[128,8]{0,1:T(8,128)}, u32[]{:S(2)}) copy-start(f32[128,8]{0,1:T(8,128)} %param.21) | copy-start | bytes 12292
  107.9 0.8 copy-start.5
  108.7 0.8 copy-start.6

commit v5 on v4

--- a/solution.py
+++ b/solution.py
@@ -16,7 +16,7 @@
 PAGE = 64
 SEG_PAGES = 8
 SEG_MOST = 2048
-STEP = 256
+STEP = 512
 META_ROWS = 16
 
 
@@ -38,13 +38,14 @@
         last = first + tok_dev - 1
         token = first + lax.broadcasted_iota(jnp.int32, (tok_dev, STEP), 0)
         column = lax.broadcasted_iota(jnp.int32, (tok_dev, STEP), 1)
-        low = jnp.zeros((tok_dev, STEP), jnp.int32)
+        narrow = token[:, :HEAD]
+        low = jnp.zeros((tok_dev, HEAD), jnp.int32)
         begin = jnp.int32(0)
         for s in range(segs):
             start = seg_ref[s]
-            low = jnp.where(token >= start, start, low)
+            low = jnp.where(narrow >= start, start, low)
             begin = jnp.where(first >= start, start, begin)
-        low_ref[...] = low
+        low_ref[...] = jnp.concatenate([low] * (STEP // HEAD), axis=1)
         query = jnp.concatenate([q_ref[block, :, h * HEAD:(h + 1) * HEAD] for h in range(QPG)], axis=0)
         den_ref[...] = jnp.zeros_like(den_ref)
         acc_ref[...] = jnp.zeros_like(acc_ref)
@@ -60,7 +61,9 @@
                 scores = lax.dot_general(query, keys, (((1,), (1,)), ((), ())), preferred_element_type=jnp.float32) * rate
                 scores = jnp.where(tiled(mask_of(step)), scores, NEG_FILL)
                 score_ref[step] = scores
-                return jnp.maximum(running, jnp.maximum(scores[:, :HEAD], scores[:, HEAD:]))
+                for part in range(STEP // HEAD):
+                    running = jnp.maximum(running, scores[:, part * HEAD : (part + 1) * HEAD])
+                return running
 
             newest = lax.fori_loop(0, steps, score, held)
             newest = jnp.broadcast_to(jnp.max(newest, axis=1, keepdims=True), (rows, HEAD))
@@ -72,8 +75,8 @@
 
             def weigh(step, ignored):
                 top = top_ref[...]
-                weights = jnp.exp2(score_ref[step] - jnp.concatenate([top, top], axis=1))
-                den_ref[...] += weights[:, :HEAD] + weights[:, HEAD:]
+                weights = jnp.exp2(score_ref[step] - jnp.concatenate([top] * (STEP // HEAD), axis=1))
+                den_ref[...] += sum([weights[:, part * HEAD : (part + 1) * HEAD] for part in range(STEP // HEAD)])
                 values = jnp.concatenate([bank[pl.ds(at, size), HEAD:] for at, size in bank_of(step)], axis=0)
                 acc_ref[...] += jnp.dot(weights.astype(jnp.bfloat16), values, preferred_element_type=jnp.float32)
                 return ignored
@@ -82,15 +85,16 @@
 
         chunk_last = first // tok_dev
         chunk_first = begin // tok_dev
-        steps = (chunk_last - chunk_first + 2) // 2
+        per = STEP // tok_dev
+        steps = (chunk_last - chunk_first + per) // per
 
         def new_chunk(step, half):
-            return chunk_last - 2 * step - 1 + half
+            return chunk_last - per * (step + 1) + 1 + half
 
         def new_bank(step):
             return [
                 (pl.multiple_of(jnp.clip(new_chunk(step, half) - opening_chunk, 0, held_chunks - 1) * tok_dev, tok_dev), tok_dev)
-                for half in range(2)
+                for half in range(per)
             ]
 
         def new_mask(step):
@@ -125,7 +129,7 @@
 
 def attention(seg_table, row_table, queries, window, bank, segs, seg_most):
     blocks, tok_dev, width = queries.shape
-    most_steps = max((seg_most + tok_dev) // tok_dev // 2 + 1, SEG_PAGES * PAGE // STEP)
+    most_steps = max(((seg_most + tok_dev) // tok_dev + STEP // tok_dev - 1) // (STEP // tok_dev), 1)
     rows = tok_dev * QPG
     return pl.pallas_call(
         functools.partial(attention_kernel, tok_dev, segs, most_steps),
@@ -359,84 +363,6 @@
     )(qkv, cached, slots)
 
 
-def project_kernel(
-    attended_ref, weight_ref, resid_ref, gain_ref, mixed_ref, normed_ref, stage, inbox, send_sems, recv_sem
-):
-    tok, ep = lax.axis_index("tok"), lax.axis_index("ep")
-    blocks, tok_dev, width = attended_ref.shape
-    number = tok * 32 + ep
-    group = lax.div(number, 4)
-    mine = group_at(ep, tok)
-    barrier = pltpu.get_barrier_semaphore()
-    for turn in range(4):
-        head = lax.rem(tok + turn, 4)
-        target = place_of(group, head)
-
-        @pl.when(jnp.logical_not((target == ep) & (head == tok)))
-        def _():
-            pl.semaphore_signal(barrier, inc=1, device_id=(head, target), device_id_type=MESH)
-
-    home = [owner_of(mine, block) for block in range(blocks)]
-    is_own = [(place[0] == tok) & (place[1] == ep) for place in home]
-    others = 4 - sum([jnp.where(flag, 1, 0) for flag in is_own])
-    pl.semaphore_wait(barrier, others)
-
-    def copy(block):
-        return pltpu.make_async_remote_copy(
-            src_ref=stage.at[block], dst_ref=inbox.at[tok], send_sem=send_sems.at[block], recv_sem=recv_sem,
-            device_id=home[block], device_id_type=MESH,
-        )
-
-    for block in range(blocks):
-        stage[block] = jnp.dot(
-            attended_ref[block], weight_ref[...], preferred_element_type=jnp.float32
-        ).astype(jnp.bfloat16)
-
-        @pl.when(is_own[block])
-        def _():
-            pltpu.make_async_copy(stage.at[block], inbox.at[tok], recv_sem).start()
-
-        @pl.when(jnp.logical_not(is_own[block]))
-        def _():
-            copy(block).start()
-
-    pltpu.make_async_copy(inbox, inbox, recv_sem).wait()
-    added = resid_ref[...].astype(jnp.float32)
-    for head in range(4):
-        added = added + inbox[head].astype(jnp.float32)
-    mixed = added.astype(jnp.bfloat16)
-    mixed_ref[...] = mixed
-    wide = mixed.astype(jnp.float32)
-    level = lax.rsqrt(jnp.mean(wide * wide, axis=-1, keepdims=True) + NORM_EPS)
-    normed_ref[...] = (wide * level * gain_ref[...]).astype(jnp.bfloat16)
-    for block in range(blocks):
-
-        @pl.when(jnp.logical_not(is_own[block]))
-        def _():
-            copy(block).wait_send()
-
-
-def project(attended, weight, resid, gain):
-    blocks, tok_dev, width = attended.shape
-    out = weight.shape[1]
-    vmem = pl.BlockSpec(memory_space=pltpu.VMEM)
-    return pl.pallas_call(
-        project_kernel,
-        out_shape=(jax.ShapeDtypeStruct(resid.shape, jnp.bfloat16),) * 2,
-        in_specs=[vmem] * 4,
-        out_specs=(vmem, vmem),
-        scratch_shapes=[
-            pltpu.VMEM((blocks, tok_dev, out), jnp.bfloat16),
-            pltpu.VMEM((4, tok_dev, out), jnp.bfloat16),
-            pltpu.SemaphoreType.DMA((blocks,)),
-            pltpu.SemaphoreType.DMA,
-        ],
-        compiler_params=pltpu.CompilerParams(collective_id=2, has_side_effects=True, vmem_limit_bytes=40 << 20),
-        cost_estimate=pl.CostEstimate(flops=2 * blocks * tok_dev * width * out, bytes_accessed=40 << 20, transcendentals=0),
-        name="project",
-    )(attended, weight, resid, gain[None, :])
-
-
 CAP = 16
 SIDE = 4
 PLANE = 32
@@ -463,16 +389,17 @@
 
 
 def routed_kernel(
-    normed_ref, mixed_ref, table_ref, gate_up_hbm, down_hbm, out_ref,
+    attended_ref, weight_ref, resid_ref, gain_ref, table_ref, gate_up_hbm, down_hbm, out_ref,
+    projected, heads, mixed_ref,
     line0, line1, line2, stage0, stage1, stage2, came0, came1, came2, back0, back1, back2,
-    part0, part1, part2, inbox0, inbox1, inbox2, sum0, sum1, sum2,
+    inbox0, inbox1, inbox2, sum0, sum1, sum2,
     gate_up, down, tables, rank, share, pick, rows_in,
     weight_sems, table_sems, line_send, line_recv, out_send, near_recv, far_recv, home_send, home_recv,
-    part_send, part_recv,
+    part_send, part_recv, head_send, head_recv,
 ):
     lines, stages, cames, backs = (line0, line1, line2), (stage0, stage1, stage2), (came0, came1, came2), (back0, back1, back2)
-    parts, inboxes, sums = (part0, part1, part2), (inbox0, inbox1, inbox2), (sum0, sum1, sum2)
-    tokens = normed_ref.shape[0]
+    inboxes, sums = (inbox0, inbox1, inbox2), (sum0, sum1, sum2)
+    tokens = resid_ref.shape[0]
     width = down.shape[0]
     devices = SIDE * PLANE
     message = SIDE * CAP
@@ -488,9 +415,19 @@
         return ignored
 
     lax.fori_loop(1, devices, greet, 0)
-    for cut, (start, size) in enumerate(CUTS):
-        lines[cut][:tokens] = normed_ref[:, start : start + size]
+    for cut in range(3):
         tables[cut, 0] = table_ref[...]
+    tok, ep = lax.axis_index("tok"), lax.axis_index("ep")
+    mine = group_at(ep, tok)
+    home = [owner_of(mine, turn) for turn in range(4)]
+    is_own = [(place[0] == tok) & (place[1] == ep) for place in home]
+
+    def project(turn):
+        projected[turn] = jnp.dot(
+            attended_ref[turn], weight_ref[...], preferred_element_type=jnp.float32
+        ).astype(jnp.bfloat16)
+
+    project(0)
     pl.semaphore_wait(barrier, devices - 1)
 
     def remote(source, place, send_sem, recv_sem, device):
@@ -509,12 +446,20 @@
             remote(
                 table_ref, tables.at[cut, turn], table_sems.at[0], table_sems.at[1], moved(line_offsets(cut, turn), 1)
             ).start()
-    for cut in range(3):
-        for turn in range(1, SIDE):
-            remote(
-                rows_of(lines[cut], 0, tokens), rows_of(lines[cut], turn * tokens, tokens),
-                line_send.at[cut], line_recv.at[cut], moved(line_offsets(cut, turn), 1),
-            ).start()
+    def head_copy(turn):
+        return remote(projected.at[turn], heads.at[tok], head_send.at[turn], head_recv, home[turn])
+
+    for turn in range(4):
+        if turn:
+            project(turn)
+
+        @pl.when(is_own[turn])
+        def _():
+            pltpu.make_async_copy(projected.at[turn], heads.at[tok], head_recv).start()
+
+        @pl.when(jnp.logical_not(is_own[turn]))
+        def _():
+            head_copy(turn).start()
 
     pltpu.make_async_copy(tables.at[:, pl.ds(0, 3)], tables.at[:, pl.ds(0, 3)], table_sems.at[1]).wait()
     before = (
@@ -541,6 +486,22 @@
             rank[at : at + PLANE, :] = jnp.where(named > 0.0, earlier, -1.0)
             share[at : at + PLANE, :] = owed
 
+    pltpu.make_async_copy(heads, heads, head_recv).wait()
+    added = resid_ref[...].astype(jnp.float32)
+    for head in range(4):
+        added = added + heads[head].astype(jnp.float32)
+    mixed_ref[...] = added.astype(jnp.bfloat16)
+    wide = mixed_ref[...].astype(jnp.float32)
+    level = lax.rsqrt(jnp.mean(wide * wide, axis=-1, keepdims=True) + NORM_EPS)
+    for cut, (start, size) in enumerate(CUTS):
+        part = mixed_ref[:, start : start + size].astype(jnp.float32)
+        lines[cut][:tokens] = (part * level * gain_ref[:, start : start + size]).astype(jnp.bfloat16)
+        for turn in range(1, SIDE):
+            remote(
+                rows_of(lines[cut], 0, tokens), rows_of(lines[cut], turn * tokens, tokens),
+                line_send.at[cut], line_recv.at[cut], moved(line_offsets(cut, turn), 1),
+            ).start()
+
     slot = lax.broadcasted_iota(jnp.int32, (CAP, tokens), 0).astype(jnp.float32)
 
     def choose(cut, core, turn, weighted):
@@ -594,6 +555,7 @@
 
     for cut in range(3):
         settle(lines[cut], 3 * tokens, line_recv.at[cut])
+        settle(lines[cut], 3 * tokens, line_send.at[cut])
     lax.fori_loop(0, 2, dispatch, 0)
     load_gate_up.wait()
     load_down.wait()
@@ -680,10 +642,10 @@
 
             @pl.when(core == 1)
             def _():
-                parts[cut][...] = sums[cut][...].astype(jnp.bfloat16)
+                lines[cut][...] = sums[cut][...].astype(jnp.bfloat16)
                 for turn in range(1, SIDE):
                     remote(
-                        rows_of(parts[cut], turn * tokens, tokens), rows_of(inboxes[cut], turn * tokens, tokens),
+                        rows_of(lines[cut], turn * tokens, tokens), rows_of(inboxes[cut], turn * tokens, tokens),
                         part_send.at[cut], part_recv.at[cut], moved(line_offsets(cut, turn), -1),
                     ).start()
 
@@ -698,14 +660,18 @@
         out_ref[:, start : start + size] = total.astype(jnp.bfloat16)
     pltpu.make_async_copy(tables.at[:, pl.ds(0, 3)], tables.at[:, pl.ds(0, 3)], table_sems.at[0]).wait()
     for cut in range(3):
-        settle(lines[cut], 3 * tokens, line_send.at[cut])
         settle(stages[cut], (PLANE - 1) * message, out_send.at[cut])
         settle(stages[cut], (PLANE - 1) * message, home_send.at[cut])
         settle(lines[cut], 3 * tokens, part_send.at[cut])
-
-
-def routed_experts(normed, mixed, routes, probs, gate_up, down):
-    tokens, width = normed.shape
+    for turn in range(4):
+
+        @pl.when(jnp.logical_not(is_own[turn]))
+        def _():
+            head_copy(turn).wait_send()
+
+
+def routed_experts(attended, weight, resid, gain, routes, probs, gate_up, down):
+    tokens, width = resid.shape
     vmem = pl.BlockSpec(memory_space=pltpu.VMEM)
     kept = pl.BlockSpec(memory_space=pl.ANY)
     slots = SIDE * PLANE * CAP
@@ -717,14 +683,18 @@
 
     return pl.pallas_call(
         routed_kernel,
-        out_shape=jax.ShapeDtypeStruct(mixed.shape, jnp.bfloat16),
-        in_specs=[vmem] * 3 + [kept] * 2,
+        out_shape=jax.ShapeDtypeStruct(resid.shape, jnp.bfloat16),
+        in_specs=[vmem] * 5 + [kept] * 2,
         out_specs=vmem,
-        scratch_shapes=each(SIDE * tokens, jnp.bfloat16)
+        scratch_shapes=[
+            pltpu.VMEM((4, tokens, width), jnp.bfloat16),
+            pltpu.VMEM((4, tokens, width), jnp.bfloat16),
+            pltpu.VMEM((tokens, width), jnp.bfloat16),
+        ]
+        + each(SIDE * tokens, jnp.bfloat16)
         + each(slots, jnp.bfloat16)
         + each(slots, jnp.bfloat16)
         + each(slots, jnp.bfloat16)
-        + each(SIDE * tokens, jnp.bfloat16)
         + each(SIDE * tokens, jnp.bfloat16)
         + each(SIDE * tokens, jnp.float32)
         + [
@@ -746,11 +716,13 @@
             pltpu.SemaphoreType.DMA((3, 2)),
             pltpu.SemaphoreType.DMA((3,)),
             pltpu.SemaphoreType.DMA((3,)),
+            pltpu.SemaphoreType.DMA((4,)),
+            pltpu.SemaphoreType.DMA,
         ],
-        compiler_params=pltpu.CompilerParams(collective_id=0, has_side_effects=True, vmem_limit_bytes=58 << 20),
+        compiler_params=pltpu.CompilerParams(collective_id=0, has_side_effects=True, vmem_limit_bytes=62 << 20),
         cost_estimate=pl.CostEstimate(flops=flops, bytes_accessed=6 * slots * width * 2, transcendentals=0),
         name="routed_experts",
-    )(normed, mixed, table, gate_up, down)
+    )(attended, weight, resid, gain[None, :], table, gate_up, down)
 
 
 def on_device(
@@ -788,8 +760,7 @@
     first_tokens = (group_at(lax.axis_index("ep"), lax.axis_index("tok")) * blocks + jnp.arange(blocks, dtype=jnp.int32)) * tok_dev
     seg_table = jnp.concatenate([seg_ends - seg_lengths, seg_ends, cache_age, first_tokens]).astype(jnp.int32)
     attended = attention(seg_table, row_table, queries, window, bank, seg_count, SEG_MOST)
-    mixed, normed = project(attended, w_out, resid, norm_gain)
-    return routed_experts(normed, mixed, routes, route_probs, w_gate_up, w_down)
+    return routed_experts(attended, w_out, resid, norm_gain, routes, route_probs, w_gate_up, w_down)
 
 
 def solution(mesh):

time: 311 us -> 304 us (0.977)
  Pallas kernels: 295 us -> 289 us
    pallas_call x2 -> x1, Pallas kernels: 226 us -> 223 us  [routed_experts(): pl.pallas_call(routed_kernel, out_shape=jax.ShapeDtypeStruct(resid.shape,...]
    pallas_call x1, Pallas kernels: 19.2 us -> 16 us  [attention(): pl.pallas_call(functools.partial(attention_kernel, tok_dev, segs, most_st...]
where the time goes in v5:
time: 304 us; the launch traced here: 300 us
  Pallas kernels  289 us (95%)
  local copies, waits for them, and re-layouts  7.84 us (3%)
    pallas_call x1, Pallas kernels, routed_experts(): pl.pallas_call(routed_kernel, out_shape=jax.ShapeDtypeStruct(resid.shape,...  223 us
    pallas_call x1, Pallas kernels, exchange(): pl.pallas_call(exchange_kernel, out_shape=(jax.ShapeDtypeStruct((4, tok_d...  49.9 us
    pallas_call x1, Pallas kernels, attention(): pl.pallas_call(functools.partial(attention_kernel, tok_dev, segs, most_st...  16 us

profile of v5, /device:TPU:8, one launch (start us, length us, event | category | flops | bytes accessed | tf_op | source)
XLA Modules:
  0.0 299.8 jit_solution(1585875117684479478)
XLA Ops:
  0.0 0.7 copy.17
  0.8 0.1 reduce
  0.9 0.7 sub.6
  1.6 0.7 pad_add_fusion.seg_ref
  2.3 0.7 convert.5
  3.0 0.6 broadcast_in_dim.24.slots_ref
  3.6 49.9 %exchange.1 = (bf16[4,128,1024]{2,1,0:T(8,128)(2,1)}, bf16[2560,256]{1,0:T(8,128)(2,1)}, bf16[8704,256]{1,0:T(8,128)(2,1)}) custom-call(bf16[128,5120]{1,0:T(8,128)(2,1)} %qkv_ref.1, bf16[256,256]{1,0:T(8,128)(2,1)} %bitcast.10, bf16[16,256]{1,0:T(8,128)(2,1)} %broadcast_in_dim.24.slots_ref), custom_call_target="tpu_custom_call" | custom-call | bytes 83886080 | tf_op jit(solution)/shard_map/exchange/pallas_call | solution.py:338
  53.5 0.0 copy-start.3
  53.5 0.0 copy-start.4
  53.5 0.9 slice.4
  54.4 0.1 reshape.68
  54.5 0.1 broadcast_add_fusion
  54.6 0.1 add.45
  54.7 0.1 select_reduce_fusion.row_ref
  54.8 0.0 copy-start
  54.8 1.3 copy-done
  56.1 0.0 copy-start.1
  56.1 1.2 copy-done.1
  57.4 16.0 %attend.1.attended_ref = bf16[4,128,1024]{2,1,0:T(8,128)(2,1)S(1)} custom-call(s32[52]{0:T(128)S(1)} %pad_add_fusion.seg_ref, s32[128]{0:T(128)S(1)} %select_reduce_fusion.row_ref, bf16[4,128,1024]{2,1,0:T(8,128)(2,1)S(1)} %copy-done.1, bf16[2560,256]{1,0:T(8,128)(2,1)S(1)} %copy-done, bf16[8704,256]{1,0:T(8,128)(2,1)} %get-tuple-element.8.bank_ref), custom_call_target="tpu_custom_call" | custom-call | tf_op jit(solution)/shard_map/attend/pallas_call | solution.py:134
  73.3 0.0 copy-start.2
  73.3 1.0 copy-done.2
  74.3 0.0 copy-done.3
  74.3 0.0 copy-done.4
  74.3 0.6 pad_maximum_fusion.table_ref
  74.9 223.0 %routed_experts.1 = bf16[128,2048]{1,0:T(8,128)(2,1)} custom-call(bf16[4,128,1024]{2,1,0:T(8,128)(2,1)} %copy-done.2, bf16[1024,2048]{1,0:T(8,128)(2,1)} %weight_ref.1, bf16[128,2048]{1,0:T(8,128)(2,1)} %resid_ref.1, f32[1,2048]{1,0:T(1,128)} %bitcast.13, f32[16,128]{1,0:T(8,128)} %pad_maximum_fusion.table_ref, bf16[1,2048,1536]{2,1,0:T(8,128)(2,1)} %gate_up_hbm.1, ...), custom_call_target="tpu_custom_call" | custom-call | flops 21474836480 | bytes 50331648 | tf_op jit(solution)/shard_map/routed_experts/pallas_call | solution.py:684
  298.0 1.9 copy.22
  (7 shorter events, 0.1 us)
Async XLA Ops:
  53.5 20.8 %copy-start.3 = (s32[128,8]{0,1:T(8,128)S(1)}, s32[128,8]{0,1:T(8,128)}, u32[]{:S(2)}) copy-start(s32[128,8]{0,1:T(8,128)} %param.20) | copy-start | bytes 12292
  53.5 20.8 %copy-start.4 = (f32[128,8]{0,1:T(8,128)S(1)}, f32[128,8]{0,1:T(8,128)}, u32[]{:S(2)}) copy-start(f32[128,8]{0,1:T(8,128)} %param.21) | copy-start | bytes 12292
  54.8 1.3 copy-start
  56.1 1.2 copy-start.1
  73.3 1.0 copy-start.2

commit v6 on v5

--- a/solution.py
+++ b/solution.py
@@ -24,7 +24,20 @@
 NORM_EPS = 1e-06
 
 
-def attention_kernel(tok_dev, segs, most_steps, seg_ref, row_ref, q_ref, window_ref, bank_ref, out_ref, score_ref, low_ref, top_ref, den_ref, acc_ref):
+def attention_kernel(tok_dev, segs, lengths_ref, age_ref, row_ref, q_hbm, window_hbm, bank_hbm, out_ref, q_ref, window_ref, bank_ref, load_sems, seg_ref, score_ref, low_ref, top_ref, den_ref, acc_ref):
+    load_q = pltpu.make_async_copy(q_hbm, q_ref, load_sems.at[0])
+    load_window = pltpu.make_async_copy(window_hbm, window_ref, load_sems.at[1])
+    load_bank = pltpu.make_async_copy(bank_hbm, bank_ref, load_sems.at[2])
+    load_q.start()
+    load_window.start()
+    load_bank.start()
+    begins = jnp.int32(0)
+    for s in range(segs):
+        seg_ref[s] = begins
+        begins = begins + lengths_ref[s]
+        seg_ref[segs + s] = begins
+        seg_ref[2 * segs + s] = age_ref[s]
+    seg_ref[3 * segs] = group_at(lax.axis_index("ep"), lax.axis_index("tok")) * q_ref.shape[0] * tok_dev
     rows = tok_dev * QPG
     held_chunks = window_ref.shape[0] // tok_dev
     opening_chunk = seg_ref[3 * segs] // tok_dev - (held_chunks - q_ref.shape[0])
@@ -34,7 +47,7 @@
         return jnp.concatenate([mask] * QPG, axis=0)
 
     def one_block(block, carry):
-        first = seg_ref[3 * segs + block]
+        first = seg_ref[3 * segs] + block * tok_dev
         last = first + tok_dev - 1
         token = first + lax.broadcasted_iota(jnp.int32, (tok_dev, STEP), 0)
         column = lax.broadcasted_iota(jnp.int32, (tok_dev, STEP), 1)
@@ -117,6 +130,10 @@
                 region(bank_ref, (age + STEP - 1) // STEP, page_bank, page_mask, False)
             return ignored
 
+        @pl.when(block == 0)
+        def _():
+            load_bank.wait()
+
         lax.fori_loop(0, segs, cached, 0)
         total = jnp.sum(den_ref[...], axis=1, keepdims=True)
         result = (acc_ref[...] / total).astype(jnp.bfloat16)
@@ -124,28 +141,35 @@
             out_ref[block, :, h * HEAD:(h + 1) * HEAD] = result[h * tok_dev:(h + 1) * tok_dev]
         return carry
 
+    load_q.wait()
+    load_window.wait()
     lax.fori_loop(0, q_ref.shape[0], one_block, 0)
 
 
-def attention(seg_table, row_table, queries, window, bank, segs, seg_most):
+def attention(seg_lengths, cache_age, row_table, queries, window, bank, segs, seg_most):
     blocks, tok_dev, width = queries.shape
     most_steps = max(((seg_most + tok_dev) // tok_dev + STEP // tok_dev - 1) // (STEP // tok_dev), 1)
     rows = tok_dev * QPG
     return pl.pallas_call(
-        functools.partial(attention_kernel, tok_dev, segs, most_steps),
+        functools.partial(attention_kernel, tok_dev, segs),
         out_shape=jax.ShapeDtypeStruct(queries.shape, jnp.bfloat16),
-        in_specs=[pl.BlockSpec(memory_space=pltpu.SMEM)] * 2 + [pl.BlockSpec(memory_space=pltpu.VMEM)] * 3,
+        in_specs=[pl.BlockSpec(memory_space=pltpu.SMEM)] * 3 + [pl.BlockSpec(memory_space=pl.ANY)] * 3,
         out_specs=pl.BlockSpec(memory_space=pltpu.VMEM),
         scratch_shapes=[
+            pltpu.VMEM(queries.shape, jnp.bfloat16),
+            pltpu.VMEM(window.shape, jnp.bfloat16),
+            pltpu.VMEM(bank.shape, jnp.bfloat16),
+            pltpu.SemaphoreType.DMA((3,)),
+            pltpu.SMEM((3 * segs + 1,), jnp.int32),
             pltpu.VMEM((most_steps, rows, STEP), jnp.float32),
             pltpu.VMEM((tok_dev, STEP), jnp.int32),
             pltpu.VMEM((rows, HEAD), jnp.float32),
             pltpu.VMEM((rows, HEAD), jnp.float32),
             pltpu.VMEM((rows, HEAD), jnp.float32),
         ],
-        compiler_params=pltpu.CompilerParams(vmem_limit_bytes=48 << 20),
+        compiler_params=pltpu.CompilerParams(vmem_limit_bytes=62 << 20),
         name="attend",
-    )(seg_table, row_table, queries, window, bank)
+    )(seg_lengths, cache_age, row_table, queries, window, bank)
 
 
 MESH = pl.DeviceIdType.MESH
@@ -168,7 +192,7 @@
 
 def exchange_kernel(
     qkv_ref, cache_ref, slots_ref, query_ref, window_ref, bank_ref,
-    stage_q, stage_kv, load_sems, key_send, key_recv, query_send, query_recv, pass_send, pass_recv, own_sem, line_send, line_recv,
+    stage_q, stage_kv, stage_slots, load_sems, key_send, key_recv, query_send, query_recv, pass_send, pass_recv, own_sem, line_send, line_recv,
     plane_send, plane_recv, pair_send, pair_recv,
 ):
     tok, ep = lax.axis_index("tok"), lax.axis_index("ep")
@@ -220,7 +244,7 @@
         device = (tok, at(tall, wide, 1 - core))
         return spans(6 - 2 * turn - 2 * core), spans(5 - 2 * turn), pass_send.at[turn + 1], pass_recv.at[turn + 1], device
 
-    held, told = cache_ref.shape[0], slots_ref.shape[0]
+    held, told = cache_ref.shape[0], stage_slots.shape[0]
     piece = held + told
     cut = piece // 32 * 16
     tall, wide, core = lax.div(ep, 8), lax.rem(lax.div(ep, 2), 4), lax.rem(ep, 2)
@@ -231,8 +255,13 @@
     def part(y, x, c, start, size):
         return bank_ref.at[pl.ds(pl.multiple_of(at(y, x, c) * piece + start, 16), size)]
 
+    lane = lax.broadcasted_iota(jnp.int32, stage_slots.shape, 1)
+    listed = jnp.zeros(stage_slots.shape, jnp.float32)
+    for page in range(slots_ref.shape[0]):
+        listed = jnp.where(lane == page, slots_ref[page].astype(jnp.float32), listed)
+    stage_slots[...] = listed.astype(jnp.bfloat16)
     own_cache = pltpu.make_async_copy(cache_ref, part(tall, wide, core, 0, held), own_sem.at[0])
-    own_slots = pltpu.make_async_copy(slots_ref, part(tall, wide, core, held, told), own_sem.at[1])
+    own_slots = pltpu.make_async_copy(stage_slots, part(tall, wide, core, held, told), own_sem.at[1])
     own_cache.start()
     own_slots.start()
 
@@ -279,13 +308,8 @@
         )
     pl.semaphore_wait(barrier, 13 - jnp.where(at_home, 1, 0))
 
-    own_cache.wait()
-    own_slots.wait()
-    for copy in (key_copy, query_copy):
-        if copy is query_copy:
-            for line_copy in line_copies():
-                line_copy.start()
-        for turn in range(4):
+    def send_each(copy, turns=range(4)):
+        for turn in turns:
             source, place, send_sem, recv_sem, device = copy(turn)
             load(turn, copy is key_copy).wait()
             if turn == 0:
@@ -299,13 +323,20 @@
                     remote(source, place, send_sem, recv_sem, device).start()
             else:
                 remote(source, place, send_sem, recv_sem, device).start()
+
     own = window_ref.at[pl.ds(reach * span, span)]
+    send_each(key_copy)
+    own_cache.wait()
+    own_slots.wait()
+    for line_copy in line_copies():
+        line_copy.start()
     pltpu.make_async_copy(own, own, key_recv).wait()
     for turn in range(1, 3):
         remote(*pass_copy(turn)).start()
     settle(3 * piece, line_recv)
     for plane_copy in plane_copies():
         plane_copy.start()
+    send_each(query_copy)
     settle(12 * piece, plane_recv)
     for pair_copy in pair_copies():
         pair_copy.start()
@@ -340,13 +371,14 @@
         out_shape=(
             jax.ShapeDtypeStruct((4, tok_dev, QPG * HEAD), jnp.bfloat16),
             jax.ShapeDtypeStruct(((reach + 1) * 4 * tok_dev, 2 * HEAD), jnp.bfloat16),
-            jax.ShapeDtypeStruct((32 * (cached.shape[0] + slots.shape[0]), 2 * HEAD), jnp.bfloat16),
+            jax.ShapeDtypeStruct((32 * (cached.shape[0] + META_ROWS), 2 * HEAD), jnp.bfloat16),
         ),
-        in_specs=[kept] * 3,
+        in_specs=[kept] * 2 + [pl.BlockSpec(memory_space=pltpu.SMEM)],
         out_specs=(kept,) * 3,
         scratch_shapes=[
             pltpu.VMEM((4, tok_dev, QPG * HEAD), jnp.bfloat16),
             pltpu.VMEM((4, tok_dev, 2 * HEAD), jnp.bfloat16),
+            pltpu.VMEM((META_ROWS, 2 * HEAD), jnp.bfloat16),
             pltpu.SemaphoreType.DMA((8,)),
             pltpu.SemaphoreType.DMA((4,)),
             pltpu.SemaphoreType.DMA,
@@ -389,8 +421,8 @@
 
 
 def routed_kernel(
-    attended_ref, weight_ref, resid_ref, gain_ref, table_ref, gate_up_hbm, down_hbm, out_ref,
-    projected, heads, mixed_ref,
+    attended_hbm, weight_hbm, resid_ref, gain_ref, table_ref, gate_up_hbm, down_hbm, out_ref,
+    attended_ref, weight_ref, projected, heads, mixed_ref,
     line0, line1, line2, stage0, stage1, stage2, came0, came1, came2, back0, back1, back2,
     inbox0, inbox1, inbox2, sum0, sum1, sum2,
     gate_up, down, tables, rank, share, pick, rows_in,
@@ -403,10 +435,12 @@
     width = down.shape[0]
     devices = SIDE * PLANE
     message = SIDE * CAP
+    load_attended = pltpu.make_async_copy(attended_hbm, attended_ref, weight_sems.at[2])
+    load_weight = pltpu.make_async_copy(weight_hbm, weight_ref, weight_sems.at[3])
+    load_attended.start()
+    load_weight.start()
     load_gate_up = pltpu.make_async_copy(gate_up_hbm.at[0], gate_up, weight_sems.at[0])
     load_down = pltpu.make_async_copy(down_hbm.at[0], down, weight_sems.at[1])
-    load_gate_up.start()
-    load_down.start()
     barrier = pltpu.get_barrier_semaphore()
 
     def greet(step, ignored):
@@ -427,6 +461,10 @@
             attended_ref[turn], weight_ref[...], preferred_element_type=jnp.float32
         ).astype(jnp.bfloat16)
 
+    load_attended.wait()
+    load_weight.wait()
+    load_gate_up.start()
+    load_down.start()
     project(0)
     pl.semaphore_wait(barrier, devices - 1)
 
@@ -496,7 +534,8 @@
     for cut, (start, size) in enumerate(CUTS):
         part = mixed_ref[:, start : start + size].astype(jnp.float32)
         lines[cut][:tokens] = (part * level * gain_ref[:, start : start + size]).astype(jnp.bfloat16)
-        for turn in range(1, SIDE):
+    for turn in range(1, SIDE):
+        for cut in range(3):
             remote(
                 rows_of(lines[cut], 0, tokens), rows_of(lines[cut], turn * tokens, tokens),
                 line_send.at[cut], line_recv.at[cut], moved(line_offsets(cut, turn), 1),
@@ -535,23 +574,17 @@
         lax.fori_loop(0, SIDE, one_shard, 0)
 
     def dispatch(core, ignored):
-        fill(2, core)
-
-        def send_far(j, inner):
+        for cut in range(3):
+            fill(cut, core)
+
+        def send_all(j, inner):
+            chunk = core * 4 + lax.div(j, 4)
             send(2, core * 16 + j, far_recv.at[core])
-            return inner
-
-        lax.fori_loop(0, 16, send_far, 0)
-        fill(0, core)
-        fill(1, core)
-
-        def send_near(j, inner):
-            chunk = core * 4 + lax.div(j, 4)
             send(0, core * 16 + j, near_recv.at[0, chunk])
             send(1, core * 16 + j, near_recv.at[1, chunk])
             return inner
 
-        return lax.fori_loop(0, 16, send_near, ignored)
+        return lax.fori_loop(0, 16, send_all, ignored)
 
     for cut in range(3):
         settle(lines[cut], 3 * tokens, line_recv.at[cut])
@@ -601,20 +634,14 @@
             slab1(chunk, j)[...] = made[j * CAP : (j + 1) * CAP, 768:1408]
             slab2(chunk, j)[...] = made[j * CAP : (j + 1) * CAP, 1408:2048]
 
-        def give_near(j, inner):
-            give(0, chunk * 4 + j)
-            give(1, chunk * 4 + j)
-            return inner
-
-        lax.fori_loop(0, 4, give_near, 0)
-
         @pl.when(lax.rem(chunk, 4) == 3)
         def _():
-            def give_far(j, inner):
-                give(2, lax.div(chunk, 4) * 16 + j)
+            def give_all(j, inner):
+                for cut in (2, 0, 1):
+                    give(cut, lax.div(chunk, 4) * 16 + j)
                 return inner
 
-            lax.fori_loop(0, 16, give_far, 0)
+            lax.fori_loop(0, 16, give_all, 0)
 
         return ignored
 
@@ -684,9 +711,11 @@
     return pl.pallas_call(
         routed_kernel,
         out_shape=jax.ShapeDtypeStruct(resid.shape, jnp.bfloat16),
-        in_specs=[vmem] * 5 + [kept] * 2,
+        in_specs=[kept] * 2 + [vmem] * 3 + [kept] * 2,
         out_specs=vmem,
         scratch_shapes=[
+            pltpu.VMEM(attended.shape, jnp.bfloat16),
+            pltpu.VMEM(weight.shape, jnp.bfloat16),
             pltpu.VMEM((4, tokens, width), jnp.bfloat16),
             pltpu.VMEM((4, tokens, width), jnp.bfloat16),
             pltpu.VMEM((tokens, width), jnp.bfloat16),
@@ -705,7 +734,7 @@
             pltpu.VMEM((3 * SIDE * PLANE, tokens), jnp.float32),
             pltpu.VMEM((16 * CAP, tokens), jnp.bfloat16),
             pltpu.VMEM((16 * CAP, width), jnp.bfloat16),
-            pltpu.SemaphoreType.DMA((2,)),
+            pltpu.SemaphoreType.DMA((4,)),
             pltpu.SemaphoreType.DMA((2,)),
             pltpu.SemaphoreType.DMA((3,)),
             pltpu.SemaphoreType.DMA((3,)),
@@ -743,11 +772,8 @@
     tok_dev = resid.shape[0]
     seg_count = seg_lengths.shape[0]
     page_count = cache_kv.shape[0]
-    slots = jnp.broadcast_to(
-        jnp.pad(page_slot, (0, 2 * HEAD - page_count))[None, :], (META_ROWS, 2 * HEAD)
-    ).astype(jnp.bfloat16)
     bank_rows = page_count * PAGE + META_ROWS
-    queries, window, bank = exchange(qkv, cache_kv.reshape(page_count * PAGE, 2 * HEAD), slots)
+    queries, window, bank = exchange(qkv, cache_kv.reshape(page_count * PAGE, 2 * HEAD), page_slot)
     held = bank.reshape(ep_count, bank_rows, 2 * HEAD)[:, bank_rows - 1, :page_count].astype(jnp.int32)
     slot_row = (
         jnp.arange(ep_count, dtype=jnp.int32)[:, None] * bank_rows
@@ -755,11 +781,7 @@
     )
     page_match = held.reshape(-1)[None, :] == jnp.arange(seg_count * SEG_PAGES, dtype=jnp.int32)[:, None]
     row_table = jnp.sum(jnp.where(page_match, slot_row.reshape(-1)[None, :], 0), axis=1).astype(jnp.int32)
-    seg_ends = jnp.cumsum(seg_lengths)
-    blocks = queries.shape[0]
-    first_tokens = (group_at(lax.axis_index("ep"), lax.axis_index("tok")) * blocks + jnp.arange(blocks, dtype=jnp.int32)) * tok_dev
-    seg_table = jnp.concatenate([seg_ends - seg_lengths, seg_ends, cache_age, first_tokens]).astype(jnp.int32)
-    attended = attention(seg_table, row_table, queries, window, bank, seg_count, SEG_MOST)
+    attended = attention(seg_lengths, cache_age, row_table, queries, window, bank, seg_count, SEG_MOST)
     return routed_experts(attended, w_out, resid, norm_gain, routes, route_probs, w_gate_up, w_down)
 
 

time: 304 us -> 285 us (0.938)
  Pallas kernels: 289 us -> 277 us
  local copies, waits for them, and re-layouts: 7.84 us -> 2.97 us
    pallas_call x1, Pallas kernels: 223 us -> 206 us  [routed_experts(): pl.pallas_call(routed_kernel, out_shape=jax.ShapeDtypeStruct(resid.shape,...]
    pallas_call x1, Pallas kernels: 16 us -> 24.6 us  [attention(): pl.pallas_call(functools.partial(attention_kernel, tok_dev, segs), out_sh...]
    unnamed x11 -> x5, local copies, waits for them, and re-layouts: 5.42 us -> 1.89 us
where the time goes in v6:
time: 285 us; the launch traced here: 282 us
  Pallas kernels  277 us (97%)
  local copies, waits for them, and re-layouts  2.97 us (1%)
    pallas_call x1, Pallas kernels, routed_experts(): pl.pallas_call(routed_kernel, out_shape=jax.ShapeDtypeStruct(resid.shape,...  206 us
    pallas_call x1, Pallas kernels, exchange(): pl.pallas_call(exchange_kernel, out_shape=(jax.ShapeDtypeStruct((4, tok_d...  47.2 us
    pallas_call x1, Pallas kernels, attention(): pl.pallas_call(functools.partial(attention_kernel, tok_dev, segs), out_sh...  24.6 us

profile of v6, /device:TPU:8, one launch (start us, length us, event | category | flops | bytes accessed | tf_op | source)
XLA Modules:
  0.0 281.8 jit_solution(15631387799198416106)
XLA Ops:
  0.0 47.2 %exchange.1 = (bf16[4,128,1024]{2,1,0:T(8,128)(2,1)}, bf16[2560,256]{1,0:T(8,128)(2,1)}, bf16[8704,256]{1,0:T(8,128)(2,1)}) custom-call(bf16[128,5120]{1,0:T(8,128)(2,1)} %qkv_ref.1, bf16[256,256]{1,0:T(8,128)(2,1)} %bitcast.9, s32[4]{0:T(128)} %slots_ref.1), custom_call_target="tpu_custom_call" | custom-call | bytes 83886080 | tf_op jit(solution)/shard_map/exchange/pallas_call | solution.py:369
  47.2 0.0 copy-start
  47.2 0.0 copy-start.1
  47.2 0.9 slice.4
  48.1 0.1 reshape.39
  48.2 0.1 broadcast_add_fusion
  48.3 0.1 add.23
  48.4 0.6 select_reduce_fusion.row_ref
  49.0 24.6 %attend.1.attended_hbm = bf16[4,128,1024]{2,1,0:T(8,128)(2,1)} custom-call(s32[16]{0:T(128)} %lengths_ref.1, s32[16]{0:T(128)} %age_ref.1, s32[128]{0:T(128)} %select_reduce_fusion.row_ref, bf16[4,128,1024]{2,1,0:T(8,128)(2,1)} %get-tuple-element.9.q_hbm, bf16[2560,256]{1,0:T(8,128)(2,1)} %get-tuple-element.10.window_hbm, ...), custom_call_target="tpu_custom_call" | custom-call | tf_op jit(solution)/shard_map/attend/pallas_call | solution.py:153
  73.7 0.0 copy-done
  73.7 0.0 copy-done.1
  73.7 0.6 pad_maximum_fusion.table_ref
  74.3 205.6 %routed_experts.1 = bf16[128,2048]{1,0:T(8,128)(2,1)} custom-call(bf16[4,128,1024]{2,1,0:T(8,128)(2,1)} %attend.1.attended_hbm, bf16[1024,2048]{1,0:T(8,128)(2,1)} %weight_hbm.1, bf16[128,2048]{1,0:T(8,128)(2,1)} %resid_ref.1, f32[1,2048]{1,0:T(1,128)} %bitcast.11, f32[16,128]{1,0:T(8,128)} %pad_maximum_fusion.table_ref, bf16[1,2048,1536]{2,1,0:T(8,128)(2,1)} %gate_up_hbm.1, ...), custom_call_target="tpu_custom_call" | custom-call | flops 21474836480 | bytes 50331648 | tf_op jit(solution)/shard_map/routed_experts/pallas_call | solution.py:711
  279.9 1.9 copy.19
  (4 shorter events, 0.0 us)
Async XLA Ops:
  47.2 26.5 %copy-start = (s32[128,8]{0,1:T(8,128)S(1)}, s32[128,8]{0,1:T(8,128)}, u32[]{:S(2)}) copy-start(s32[128,8]{0,1:T(8,128)} %param.20) | copy-start | bytes 12292
  47.2 26.5 %copy-start.1 = (f32[128,8]{0,1:T(8,128)S(1)}, f32[128,8]{0,1:T(8,128)}, u32[]{:S(2)}) copy-start(f32[128,8]{0,1:T(8,128)} %param.21) | copy-start | bytes 12292

commit v7 on v6

--- a/solution.py
+++ b/solution.py
@@ -416,6 +416,10 @@
     return ((0, inner, outer, core), (inner, 0, outer, core), (outer, inner, 0, core))[cut]
 
 
+def mixed_order(j):
+    return lax.rem(j, 4) * 4 + lax.rem(lax.div(j, 4) + j, 4)
+
+
 def line_offsets(cut, turn):
     return tuple(turn if axis == cut else 0 for axis in range(3)) + (0,)
 
@@ -534,7 +538,7 @@
     for cut, (start, size) in enumerate(CUTS):
         part = mixed_ref[:, start : start + size].astype(jnp.float32)
         lines[cut][:tokens] = (part * level * gain_ref[:, start : start + size]).astype(jnp.bfloat16)
-    for turn in range(1, SIDE):
+    for turn in (1, 3, 2):
         for cut in range(3):
             remote(
                 rows_of(lines[cut], 0, tokens), rows_of(lines[cut], turn * tokens, tokens),
@@ -577,7 +581,8 @@
         for cut in range(3):
             fill(cut, core)
 
-        def send_all(j, inner):
+        def send_all(order, inner):
+            j = mixed_order(order)
             chunk = core * 4 + lax.div(j, 4)
             send(2, core * 16 + j, far_recv.at[core])
             send(0, core * 16 + j, near_recv.at[0, chunk])
@@ -636,9 +641,9 @@
 
         @pl.when(lax.rem(chunk, 4) == 3)
         def _():
-            def give_all(j, inner):
+            def give_all(order, inner):
                 for cut in (2, 0, 1):
-                    give(cut, lax.div(chunk, 4) * 16 + j)
+                    give(cut, lax.div(chunk, 4) * 16 + mixed_order(order))
                 return inner
 
             lax.fori_loop(0, 16, give_all, 0)

time: 285 us -> 283 us (level)
    pallas_call x1, Pallas kernels: 24.6 us -> 15 us  [attention(): pl.pallas_call(functools.partial(attention_kernel, tok_dev, segs), out_sh...]
    pallas_call x1, Pallas kernels: 206 us -> 212 us  [routed_experts(): pl.pallas_call(routed_kernel, out_shape=jax.ShapeDtypeStruct(resid.shape,...]
where the time goes in v7:
time: 283 us; the launch traced here: 279 us
  Pallas kernels  275 us (97%)
  local copies, waits for them, and re-layouts  2.97 us (1%)
    pallas_call x1, Pallas kernels, routed_experts(): pl.pallas_call(routed_kernel, out_shape=jax.ShapeDtypeStruct(resid.shape,...  212 us
    pallas_call x1, Pallas kernels, exchange(): pl.pallas_call(exchange_kernel, out_shape=(jax.ShapeDtypeStruct((4, tok_d...  47.2 us
    pallas_call x1, Pallas kernels, attention(): pl.pallas_call(functools.partial(attention_kernel, tok_dev, segs), out_sh...  15 us

profile of v7, /device:TPU:8, one launch (start us, length us, event | category | flops | bytes accessed | tf_op | source)
XLA Modules:
  0.0 279.0 jit_solution(5238816234999091170)
XLA Ops:
  0.0 47.2 %exchange.1 = (bf16[4,128,1024]{2,1,0:T(8,128)(2,1)}, bf16[2560,256]{1,0:T(8,128)(2,1)}, bf16[8704,256]{1,0:T(8,128)(2,1)}) custom-call(bf16[128,5120]{1,0:T(8,128)(2,1)} %qkv_ref.1, bf16[256,256]{1,0:T(8,128)(2,1)} %bitcast.9, s32[4]{0:T(128)} %slots_ref.1), custom_call_target="tpu_custom_call" | custom-call | bytes 83886080 | tf_op jit(solution)/shard_map/exchange/pallas_call | solution.py:369
  47.2 0.0 copy-start
  47.2 0.0 copy-start.1
  47.2 0.9 slice.4
  48.1 0.1 reshape.39
  48.2 0.1 broadcast_add_fusion
  48.3 0.1 add.23
  48.4 0.6 select_reduce_fusion.row_ref
  49.0 15.0 %attend.1.attended_hbm = bf16[4,128,1024]{2,1,0:T(8,128)(2,1)} custom-call(s32[16]{0:T(128)} %lengths_ref.1, s32[16]{0:T(128)} %age_ref.1, s32[128]{0:T(128)} %select_reduce_fusion.row_ref, bf16[4,128,1024]{2,1,0:T(8,128)(2,1)} %get-tuple-element.9.q_hbm, bf16[2560,256]{1,0:T(8,128)(2,1)} %get-tuple-element.10.window_hbm, ...), custom_call_target="tpu_custom_call" | custom-call | tf_op jit(solution)/shard_map/attend/pallas_call | solution.py:153
  64.1 0.0 copy-done
  64.1 0.0 copy-done.1
  64.1 0.6 pad_maximum_fusion.table_ref
  64.7 212.4 %routed_experts.1 = bf16[128,2048]{1,0:T(8,128)(2,1)} custom-call(bf16[4,128,1024]{2,1,0:T(8,128)(2,1)} %attend.1.attended_hbm, bf16[1024,2048]{1,0:T(8,128)(2,1)} %weight_hbm.1, bf16[128,2048]{1,0:T(8,128)(2,1)} %resid_ref.1, f32[1,2048]{1,0:T(1,128)} %bitcast.11, f32[16,128]{1,0:T(8,128)} %pad_maximum_fusion.table_ref, bf16[1,2048,1536]{2,1,0:T(8,128)(2,1)} %gate_up_hbm.1, ...), custom_call_target="tpu_custom_call" | custom-call | flops 21474836480 | bytes 50331648 | tf_op jit(solution)/shard_map/routed_experts/pallas_call | solution.py:716
  277.2 1.9 copy.19
  (4 shorter events, 0.0 us)
Async XLA Ops:
  47.2 16.9 %copy-start = (s32[128,8]{0,1:T(8,128)S(1)}, s32[128,8]{0,1:T(8,128)}, u32[]{:S(2)}) copy-start(s32[128,8]{0,1:T(8,128)} %param.20) | copy-start | bytes 12292
  47.2 16.9 %copy-start.1 = (f32[128,8]{0,1:T(8,128)S(1)}, f32[128,8]{0,1:T(8,128)}, u32[]{:S(2)}) copy-start(f32[128,8]{0,1:T(8,128)} %param.21) | copy-start | bytes 12292

commit v8 on v7

--- a/solution.py
+++ b/solution.py
@@ -578,18 +578,26 @@
         lax.fori_loop(0, SIDE, one_shard, 0)
 
     def dispatch(core, ignored):
-        for cut in range(3):
+        def send_one(cut, order):
+            j = mixed_order(order)
+            arrival = far_recv.at[core] if cut == 2 else near_recv.at[cut, core * 4 + lax.div(j, 4)]
+            send(cut, core * 16 + j, arrival)
+
+        for cut in (2, 0, 1):
             fill(cut, core)
 
+            def send_first(order, inner, cut=cut):
+                send_one(cut, order)
+                return inner
+
+            lax.fori_loop(0, 4, send_first, 0)
+
         def send_all(order, inner):
-            j = mixed_order(order)
-            chunk = core * 4 + lax.div(j, 4)
-            send(2, core * 16 + j, far_recv.at[core])
-            send(0, core * 16 + j, near_recv.at[0, chunk])
-            send(1, core * 16 + j, near_recv.at[1, chunk])
+            for cut in (2, 0, 1):
+                send_one(cut, order)
             return inner
 
-        return lax.fori_loop(0, 16, send_all, ignored)
+        return lax.fori_loop(4, 16, send_all, ignored)
 
     for cut in range(3):
         settle(lines[cut], 3 * tokens, line_recv.at[cut])

time: 283 us -> 283 us (level)
    pallas_call x1, Pallas kernels: 15 us -> 24.3 us  [attention(): pl.pallas_call(functools.partial(attention_kernel, tok_dev, segs), out_sh...]
    pallas_call x1, Pallas kernels: 212 us -> 204 us  [routed_experts(): pl.pallas_call(routed_kernel, out_shape=jax.ShapeDtypeStruct(resid.shape,...]
where the time goes in v8:
time: 283 us; the launch traced here: 280 us
  Pallas kernels  276 us (98%)
  local copies, waits for them, and re-layouts  2.97 us (1%)
    pallas_call x1, Pallas kernels, routed_experts(): pl.pallas_call(routed_kernel, out_shape=jax.ShapeDtypeStruct(resid.shape,...  204 us
    pallas_call x1, Pallas kernels, exchange(): pl.pallas_call(exchange_kernel, out_shape=(jax.ShapeDtypeStruct((4, tok_d...  47.2 us
    pallas_call x1, Pallas kernels, attention(): pl.pallas_call(functools.partial(attention_kernel, tok_dev, segs), out_sh...  24.3 us

profile of v8, /device:TPU:8, one launch (start us, length us, event | category | flops | bytes accessed | tf_op | source)
XLA Modules:
  0.0 280.2 jit_solution(16011579856122568301)
XLA Ops:
  0.0 47.2 %exchange.1 = (bf16[4,128,1024]{2,1,0:T(8,128)(2,1)}, bf16[2560,256]{1,0:T(8,128)(2,1)}, bf16[8704,256]{1,0:T(8,128)(2,1)}) custom-call(bf16[128,5120]{1,0:T(8,128)(2,1)} %qkv_ref.1, bf16[256,256]{1,0:T(8,128)(2,1)} %bitcast.9, s32[4]{0:T(128)} %slots_ref.1), custom_call_target="tpu_custom_call" | custom-call | bytes 83886080 | tf_op jit(solution)/shard_map/exchange/pallas_call | solution.py:369
  47.2 0.0 copy-start
  47.2 0.0 copy-start.1
  47.2 0.9 slice.4
  48.1 0.1 reshape.39
  48.2 0.1 broadcast_add_fusion
  48.3 0.1 add.23
  48.4 0.6 select_reduce_fusion.row_ref
  49.0 24.3 %attend.1.attended_hbm = bf16[4,128,1024]{2,1,0:T(8,128)(2,1)} custom-call(s32[16]{0:T(128)} %lengths_ref.1, s32[16]{0:T(128)} %age_ref.1, s32[128]{0:T(128)} %select_reduce_fusion.row_ref, bf16[4,128,1024]{2,1,0:T(8,128)(2,1)} %get-tuple-element.9.q_hbm, bf16[2560,256]{1,0:T(8,128)(2,1)} %get-tuple-element.10.window_hbm, ...), custom_call_target="tpu_custom_call" | custom-call | tf_op jit(solution)/shard_map/attend/pallas_call | solution.py:153
  73.3 0.0 copy-done
  73.4 0.0 copy-done.1
  73.4 0.6 pad_maximum_fusion.table_ref
  74.0 204.4 %routed_experts.1 = bf16[128,2048]{1,0:T(8,128)(2,1)} custom-call(bf16[4,128,1024]{2,1,0:T(8,128)(2,1)} %attend.1.attended_hbm, bf16[1024,2048]{1,0:T(8,128)(2,1)} %weight_hbm.1, bf16[128,2048]{1,0:T(8,128)(2,1)} %resid_ref.1, f32[1,2048]{1,0:T(1,128)} %bitcast.11, f32[16,128]{1,0:T(8,128)} %pad_maximum_fusion.table_ref, bf16[1,2048,1536]{2,1,0:T(8,128)(2,1)} %gate_up_hbm.1, ...), custom_call_target="tpu_custom_call" | custom-call | flops 21474836480 | bytes 50331648 | tf_op jit(solution)/shard_map/routed_experts/pallas_call | solution.py:724
  278.4 1.9 copy.19
  (4 shorter events, 0.0 us)
Async XLA Ops:
  47.2 26.1 %copy-start = (s32[128,8]{0,1:T(8,128)S(1)}, s32[128,8]{0,1:T(8,128)}, u32[]{:S(2)}) copy-start(s32[128,8]{0,1:T(8,128)} %param.20) | copy-start | bytes 12292
  47.2 26.1 %copy-start.1 = (f32[128,8]{0,1:T(8,128)S(1)}, f32[128,8]{0,1:T(8,128)}, u32[]{:S(2)}) copy-start(f32[128,8]{0,1:T(8,128)} %param.21) | copy-start | bytes 12292

commit v9 on v7

--- a/solution.py
+++ b/solution.py
@@ -491,7 +491,7 @@
     def head_copy(turn):
         return remote(projected.at[turn], heads.at[tok], head_send.at[turn], head_recv, home[turn])
 
-    for turn in range(4):
+    for turn in (0, 2, 1, 3):
         if turn:
             project(turn)
 

time: 283 us -> 285 us (level)
  Pallas kernels: 275 us -> 278 us
    pallas_call x1, Pallas kernels: 15 us -> 19 us  [attention(): pl.pallas_call(functools.partial(attention_kernel, tok_dev, segs), out_sh...]
where the time goes in v9:
time: 285 us; the launch traced here: 282 us
  Pallas kernels  278 us (98%)
  local copies, waits for them, and re-layouts  2.97 us (1%)
    pallas_call x1, Pallas kernels, routed_experts(): pl.pallas_call(routed_kernel, out_shape=jax.ShapeDtypeStruct(resid.shape,...  212 us
    pallas_call x1, Pallas kernels, exchange(): pl.pallas_call(exchange_kernel, out_shape=(jax.ShapeDtypeStruct((4, tok_d...  47.2 us
    pallas_call x1, Pallas kernels, attention(): pl.pallas_call(functools.partial(attention_kernel, tok_dev, segs), out_sh...  19 us

profile of v9, /device:TPU:8, one launch (start us, length us, event | category | flops | bytes accessed | tf_op | source)
XLA Modules:
  0.0 282.1 jit_solution(15113874827212702788)
XLA Ops:
  0.0 47.2 %exchange.1 = (bf16[4,128,1024]{2,1,0:T(8,128)(2,1)}, bf16[2560,256]{1,0:T(8,128)(2,1)}, bf16[8704,256]{1,0:T(8,128)(2,1)}) custom-call(bf16[128,5120]{1,0:T(8,128)(2,1)} %qkv_ref.1, bf16[256,256]{1,0:T(8,128)(2,1)} %bitcast.9, s32[4]{0:T(128)} %slots_ref.1), custom_call_target="tpu_custom_call" | custom-call | bytes 83886080 | tf_op jit(solution)/shard_map/exchange/pallas_call | solution.py:369
  47.2 0.0 copy-start
  47.2 0.0 copy-start.1
  47.2 0.9 slice.4
  48.1 0.1 reshape.39
  48.2 0.1 broadcast_add_fusion
  48.3 0.1 add.23
  48.4 0.6 select_reduce_fusion.row_ref
  49.0 19.0 %attend.1.attended_hbm = bf16[4,128,1024]{2,1,0:T(8,128)(2,1)} custom-call(s32[16]{0:T(128)} %lengths_ref.1, s32[16]{0:T(128)} %age_ref.1, s32[128]{0:T(128)} %select_reduce_fusion.row_ref, bf16[4,128,1024]{2,1,0:T(8,128)(2,1)} %get-tuple-element.9.q_hbm, bf16[2560,256]{1,0:T(8,128)(2,1)} %get-tuple-element.10.window_hbm, ...), custom_call_target="tpu_custom_call" | custom-call | tf_op jit(solution)/shard_map/attend/pallas_call | solution.py:153
  68.0 0.0 copy-done
  68.0 0.0 copy-done.1
  68.0 0.6 pad_maximum_fusion.table_ref
  68.6 211.5 %routed_experts.1 = bf16[128,2048]{1,0:T(8,128)(2,1)} custom-call(bf16[4,128,1024]{2,1,0:T(8,128)(2,1)} %attend.1.attended_hbm, bf16[1024,2048]{1,0:T(8,128)(2,1)} %weight_hbm.1, bf16[128,2048]{1,0:T(8,128)(2,1)} %resid_ref.1, f32[1,2048]{1,0:T(1,128)} %bitcast.11, f32[16,128]{1,0:T(8,128)} %pad_maximum_fusion.table_ref, bf16[1,2048,1536]{2,1,0:T(8,128)(2,1)} %gate_up_hbm.1, ...), custom_call_target="tpu_custom_call" | custom-call | flops 21474836480 | bytes 50331648 | tf_op jit(solution)/shard_map/routed_experts/pallas_call | solution.py:716
  280.2 1.9 copy.19
  (4 shorter events, 0.0 us)
Async XLA Ops:
  47.2 20.8 %copy-start = (s32[128,8]{0,1:T(8,128)S(1)}, s32[128,8]{0,1:T(8,128)}, u32[]{:S(2)}) copy-start(s32[128,8]{0,1:T(8,128)} %param.20) | copy-start | bytes 12292
  47.2 20.8 %copy-start.1 = (f32[128,8]{0,1:T(8,128)S(1)}, f32[128,8]{0,1:T(8,128)}, u32[]{:S(2)}) copy-start(f32[128,8]{0,1:T(8,128)} %param.21) | copy-start | bytes 12292
